TPU v7x, 128 devices: a whole 4x4x4 slice. The times are simulated.
128 devices in a mesh: grp: 4 (over x), dev: 32 (over y, z, core).
Axes of the slice: x: 4, y: 4, z: 4, core: 2. Of those that a mesh axis runs over, the one named last changes fastest.
Arguments:
- locations: float32 [128, 3, 256], P(('grp', 'dev')), may hold values from 0 to 1
- neighbours: int32 [128, 4], P(('grp', 'dev')), may hold values from -1 to 126, as said below
- observations: float32 [128, 8, 256], P(('grp', 'dev')), may hold values from -63 to 63
- noise_prec: float32 [128, 8, 256], P(('grp', 'dev')), may hold values from 0.5 to 4
Outputs:
- solution: float32 [128, 8, 256], P(('grp', 'dev'))
- residual: float32 [128, 8, 256], P(('grp', 'dev'))
Inputs may be any that keep to these rules, and one draw needn't show every extreme that they name: `neighbours`: row b holds b - 1 in slot 0 (-1 for block 0); in slot 1 a block drawn from the range from max(b - 1, 0) * 1 to b - 2, or -1 where that range is empty; in slots 2 and 3 two different blocks below min(32, max(b - 1, 0)), -1 in a slot where fewer exist. All listed blocks of a row differ.
All inputs are finite; a program needn't handle non-finite values.
Results may differ from a plain program's by a relative error of at most 0.0003.
Values sent between devices are 32-bit elements; how exact they have to be, the bound alone decides.
A program may use at most 128 MiB of HBM per device.

v0:
```python
import math

import jax
import jax.numpy as jnp
from jax import lax
from jax.sharding import PartitionSpec as P

ITERS = 2


SCALE_LENGTH = 0.5
NUGGET = 0.5
SQRT_THREE = math.sqrt(3.0)
HIGHEST = lax.Precision.HIGHEST


def from_behind(block, axis, distance):
    devices = range(lax.axis_size(axis))
    route = [(i - distance, i) for i in devices if i - distance in devices]
    return lax.ppermute(block, axis, route)


def from_root(value, axis, source):
    kept = jnp.where(lax.axis_index(axis) == source, value, 0).astype(value.dtype)
    return lax.psum(kept, axis)


def kernel_factor(point_set, point_mask, own_size):
    offsets = point_set[:, :, None] - point_set[:, None, :]
    distance = jnp.sqrt(jnp.sum(offsets * offsets, axis=0))
    scaled = SQRT_THREE / SCALE_LENGTH * distance
    covariance = (1.0 + scaled) * jnp.exp(-scaled)
    order_size = point_set.shape[1]
    identity = jnp.eye(order_size, dtype=point_set.dtype)
    diagonal_term = NUGGET * point_mask + (1.0 - point_mask)
    covariance = (
        covariance * (point_mask[:, None] * point_mask[None, :]) + identity * diagonal_term[:, None]
    )
    factor_lower = jnp.linalg.cholesky(covariance)
    unit_tail = identity[:, order_size - own_size :]
    return lax.linalg.triangular_solve(
        factor_lower, unit_tail, left_side=True, lower=True, transpose_a=True
    )


def local(locations, neighbours, observations, noise_prec):
    blocks = locations.shape[0]
    points = locations.shape[2]
    fields = observations.shape[1]
    slot_count = neighbours.shape[1]
    coarse = blocks * lax.axis_size("dev")
    first_local = (lax.axis_index(("grp", "dev")) - 1) * blocks
    slot_live = (neighbours >= 0).astype(jnp.float32)
    near_ids = neighbours[:, :2] - first_local
    near_select = (
        near_ids[:, :, None] == jnp.arange(2 * blocks, dtype=jnp.int32)[None, None, :]
    ).astype(jnp.float32)
    near_select = near_select * slot_live[:, :2, None]
    coarse_select = (
        neighbours[:, 2:, None] == jnp.arange(coarse, dtype=jnp.int32)[None, None, :]
    ).astype(jnp.float32)
    owner_flag = (lax.axis_index("grp") == 0).astype(jnp.float32)

    def fetch(packed):
        before = from_behind(packed, ("grp", "dev"), 1)
        column_rows = lax.all_gather(packed, "dev", axis=0, tiled=True)
        coarse_rows = from_root(column_rows, "grp", 0)
        near_table = jnp.concatenate([before, packed], axis=0)
        near_rows = jnp.einsum("bsn,ncp->bcsp", near_select, near_table, precision=HIGHEST)
        coarse_picked = jnp.einsum("bsn,ncp->bcsp", coarse_select, coarse_rows, precision=HIGHEST)
        slot_rows = jnp.concatenate([near_rows, coarse_picked], axis=2)
        slot_rows = slot_rows.reshape(blocks, packed.shape[1], slot_count * points)
        return jnp.concatenate([slot_rows, packed], axis=2)

    gathered_first = fetch(jnp.concatenate([locations, observations], axis=1))
    point_sets = gathered_first[:, :3]
    point_mask = jnp.concatenate(
        [jnp.repeat(slot_live, points, axis=1), jnp.ones((blocks, points), jnp.float32)], axis=1
    )
    factors = lax.map(
        lambda pair: kernel_factor(pair[0], pair[1], points), (point_sets, point_mask)
    )

    def squared_norm(field):
        return lax.psum(jnp.sum(field * field, axis=(0, 2)), ("grp", "dev"))

    solution = jnp.zeros_like(observations)
    residual = observations
    direction = observations
    norm_now = squared_norm(residual)
    for iteration in range(ITERS):
        if iteration == 0:
            gathered = gathered_first[:, 3:]
        else:
            gathered = fetch(direction)
        weighted = jnp.einsum("bvk,bkp->bvp", gathered, factors, precision=HIGHEST)
        spread = jnp.einsum("bvp,bkp->bvk", weighted, factors, precision=HIGHEST)
        own_part = spread[:, :, slot_count * points :]
        slot_parts = spread[:, :, : slot_count * points].reshape(blocks, fields, slot_count, points)
        near_back = jnp.einsum(
            "bsn,bvsp->nvp", near_select, slot_parts[:, :, :2], precision=HIGHEST
        )
        coarse_back = jnp.einsum(
            "bsn,bvsp->nvp", coarse_select, slot_parts[:, :, 2:], precision=HIGHEST
        )
        returned = from_behind(near_back[:blocks], ("grp", "dev"), -1)
        summed_rows = lax.psum(coarse_back, "grp")
        owned_rows = lax.psum_scatter(summed_rows, "dev", scatter_dimension=0, tiled=True)
        image = (
            own_part
            + near_back[blocks:]
            + returned
            + owner_flag * owned_rows
            + noise_prec * direction
        )
        product = lax.psum(jnp.sum(direction * image, axis=(0, 2)), ("grp", "dev"))
        alpha = norm_now / product
        solution = solution + alpha[None, :, None] * direction
        residual = residual - alpha[None, :, None] * image
        if iteration + 1 < ITERS:
            norm_next = squared_norm(residual)
            direction = residual + (norm_next / norm_now)[None, :, None] * direction
            norm_now = norm_next
    return (solution, residual)


def solution(mesh):
    placed = (
        P(("grp", "dev"), None, None),
        P(("grp", "dev"), None),
        P(("grp", "dev"), None, None),
        P(("grp", "dev"), None, None),
    )
    return jax.shard_map(
        local,
        mesh=mesh,
        in_specs=placed,
        out_specs=(P(("grp", "dev"), None, None), P(("grp", "dev"), None, None)),
        check_vma=False,
    )
```

profile of v0, /device:TPU:0, one launch (start us, length us, event | category | flops | bytes accessed | tf_op | source)
XLA Modules:
  0.0 989.9 jit_solution(18137867022828427077)
XLA Ops:
  9.9 27.0 %all_gather.6 = f32[32,11,256]{2,1,0:T(8,128)S(1)} all-gather(f32[1,11,256]{2,1,0:T(8,128)S(1)} %copy.58), channel_id=1, replica_groups=mesh['grp'=4,'dev'=32] {'dev'}, dimensions={0}, use_global_device_ids=true | all-gather | bytes 371712 | tf_op jit(solution)/shard_map/all_gather | solution.py:66
  42.2 37.3 %all-reduce.6.cloned.1.call-done = f32[32,11,256]{2,0,1:T(8,128)} async-done(((f32[32,11,256]{2,0,1:T(8,128)}), f32[32,11,256]{2,0,1:T(8,128)}) %all-reduce.6.cloned.1.call-update) | async-done | bytes 360464 | tf_op jit(solution)/shard_map/psum | solution.py:25
  122.4 11.7 %cholesky.280 = f32[128,128]{1,0:T(8,128)S(1)} custom-call(f32[128,128]{1,0:T(8,128)S(1)} %cholesky.733), custom_call_target="Cholesky" | custom-call | tf_op jit(solution)/shard_map/while/body/eval_jaxpr/jit(cholesky)/cholesky | solution.py:39
  151.3 11.7 %cholesky.303 = f32[128,128]{1,0:T(8,128)S(1)} custom-call(f32[128,128]{1,0:T(8,128)S(1)} %cholesky.737), custom_call_target="Cholesky" | custom-call | tf_op jit(solution)/shard_map/while/body/eval_jaxpr/jit(cholesky)/cholesky | solution.py:39
  177.5 11.7 %cholesky.328 = f32[128,128]{1,0:T(8,128)S(1)} custom-call(f32[128,128]{1,0:T(8,128)S(1)} %cholesky.742), custom_call_target="Cholesky" | custom-call | tf_op jit(solution)/shard_map/while/body/eval_jaxpr/jit(cholesky)/cholesky | solution.py:39
  204.5 12.1 %cholesky.599 = f32[128,128]{1,0:T(8,128)S(1)} custom-call(f32[128,128]{1,0:T(8,128)S(1)} %cholesky.747), custom_call_target="Cholesky" | custom-call | tf_op jit(solution)/shard_map/while/body/eval_jaxpr/jit(cholesky)/cholesky | solution.py:39
  232.0 11.7 %cholesky.618 = f32[128,128]{1,0:T(8,128)S(1)} custom-call(f32[128,128]{1,0:T(8,128)S(1)} %cholesky.752), custom_call_target="Cholesky" | custom-call | tf_op jit(solution)/shard_map/while/body/eval_jaxpr/jit(cholesky)/cholesky | solution.py:39
  259.3 11.7 %cholesky.638 = f32[128,128]{1,0:T(8,128)S(1)} custom-call(f32[128,128]{1,0:T(8,128)S(1)} %cholesky.757), custom_call_target="Cholesky" | custom-call | tf_op jit(solution)/shard_map/while/body/eval_jaxpr/jit(cholesky)/cholesky | solution.py:39
  286.2 11.9 %cholesky.658 = f32[128,128]{1,0:T(8,128)S(1)} custom-call(f32[128,128]{1,0:T(8,128)S(1)} %cholesky.762), custom_call_target="Cholesky" | custom-call | tf_op jit(solution)/shard_map/while/body/eval_jaxpr/jit(cholesky)/cholesky | solution.py:39
  313.1 11.7 %cholesky.678 = f32[128,128]{1,0:T(8,128)S(1)} custom-call(f32[128,128]{1,0:T(8,128)S(1)} %cholesky.767), custom_call_target="Cholesky" | custom-call | tf_op jit(solution)/shard_map/while/body/eval_jaxpr/jit(cholesky)/cholesky | solution.py:39
  326.1 10.3 %custom-call.105 = f32[1,128,128]{1,2,0:T(8,128)S(1)} custom-call(f32[1,128,128]{2,1,0:T(8,128)S(1)} %get-tuple-element.45), custom_call_target="InvertDiagBlocksLowerTriangular" | custom-call | tf_op jit(solution)/shard_map/while/body/eval_jaxpr/jit(cholesky)/cholesky | solution.py:39
  339.6 11.7 %cholesky.698 = f32[128,128]{1,0:T(8,128)S(1)} custom-call(f32[128,128]{1,0:T(8,128)S(1)} %cholesky.772), custom_call_target="Cholesky" | custom-call | tf_op jit(solution)/shard_map/while/body/eval_jaxpr/jit(cholesky)/cholesky | solution.py:39
  365.5 11.7 %cholesky.716 = f32[128,128]{1,0:T(8,128)S(1)} custom-call(f32[128,128]{1,0:T(8,128)S(1)} %convolution_subtract_fusion.12), custom_call_target="Cholesky" | custom-call | tf_op jit(solution)/shard_map/while/body/eval_jaxpr/jit(cholesky)/cholesky | solution.py:39
  391.5 34.9 %while.1 = (s32[]{:T(128)}, f32[1280,1280]{1,0:T(8,128)}, s32[10,2]{0,1:T(2,128)S(1)}, f32[10,128,128]{2,1,0:T(8,128)}, s32[]{:T(128)}) while((s32[]{:T(128)}, f32[1280,1280]{1,0:T(8,128)}, s32[10,2]{0,1:T(2,128)S(1)}, f32[10,128,128]{2,1,0:T(8,128)}, s32[]{:T(128)}) %tuple.60), condition=%wide.while_cond, body=%wide.while_body.sunk | while | flops 2 | bytes 132705 | solution.py:41
  426.4 99.0 %custom-call.107 = f32[10,128,128]{1,2,0:T(8,128)S(1)} custom-call(f32[10,128,128]{2,1,0:T(8,128)} %get-tuple-element.21), custom_call_target="InvertDiagBlocksLowerTriangular" | custom-call | tf_op jit(solution)/shard_map/while/body/eval_jaxpr/triangular_solve | solution.py:41
  549.5 76.5 %reduce-scatter.3.cloned.1.call-done = f32[1,8,256]{2,1,0:T(8,128)} async-done(((f32[32,8,256]{2,1,0:T(8,128)}), f32[1,8,256]{2,1,0:T(8,128)}) %reduce-scatter.3.cloned.1.call-update) | async-done | bytes 8208 | tf_op jit(solution)/shard_map/reduce_scatter | solution.py:108
  626.0 10.6 %psum.64 = f32[1,8,256]{2,1,0:T(8,128)S(1)} all-reduce(f32[1,8,256]{2,1,0:T(8,128)} %reduce-scatter.3.cloned.1.call-done), channel_id=1, replica_groups=mesh['grp'=4,'dev'=32] {'grp'}, use_global_device_ids=true, to_apply=%region_24.25 | all-reduce | flops 2048 | bytes 16384 | tf_op jit(solution)/shard_map/psum | solution.py:107
  636.8 62.4 %all-reduce.2 = (f32[8]{0:T(128)S(1)}, f32[8]{0:T(128)S(1)}) all-reduce(f32[8]{0:T(128)S(1)} %get-tuple-element.23, f32[8]{0:T(128)S(1)} %get-tuple-element.22), channel_id=1, replica_groups=mesh['grp'=4,'dev'=32] {'grp','dev'}, use_global_device_ids=true, to_apply=%region_1.2 | all-reduce | flops 16 | bytes 128 | tf_op jit(solution)/shard_map/psum | solution.py:85
  699.4 64.2 %psum.60 = f32[8]{0:T(128)S(1)} all-reduce(f32[8]{0:T(128)S(1)} %multiply_reduce_fusion.2), channel_id=1, replica_groups=mesh['grp'=4,'dev'=32] {'grp','dev'}, use_global_device_ids=true, to_apply=%region_29.30 | all-reduce | flops 8 | bytes 64 | tf_op jit(solution)/shard_map/psum | solution.py:85
  763.7 22.3 %all_gather.7 = f32[32,8,256]{2,1,0:T(8,128)S(1)} all-gather(f32[1,8,256]{2,1,0:T(8,128)S(1)} %multiply_add_fusion.1), channel_id=1, replica_groups=mesh['grp'=4,'dev'=32] {'dev'}, dimensions={0}, use_global_device_ids=true | all-gather | bytes 270336 | tf_op jit(solution)/shard_map/all_gather | solution.py:66
  790.2 36.5 %all-reduce.8.cloned.1.call-done = f32[32,8,256]{2,0,1:T(8,128)} async-done(((f32[32,8,256]{2,0,1:T(8,128)}), f32[32,8,256]{2,0,1:T(8,128)}) %all-reduce.8.cloned.1.call-update) | async-done | bytes 262160 | tf_op jit(solution)/shard_map/psum | solution.py:25
  832.8 76.6 %reduce-scatter.5.cloned.1.call-done = f32[1,8,256]{2,1,0:T(8,128)} async-done(((f32[32,8,256]{2,1,0:T(8,128)}), f32[1,8,256]{2,1,0:T(8,128)}) %reduce-scatter.5.cloned.1.call-update) | async-done | bytes 8208 | tf_op jit(solution)/shard_map/reduce_scatter | solution.py:108
  909.3 10.6 %psum.65 = f32[1,8,256]{2,1,0:T(8,128)S(1)} all-reduce(f32[1,8,256]{2,1,0:T(8,128)} %reduce-scatter.5.cloned.1.call-done), channel_id=1, replica_groups=mesh['grp'=4,'dev'=32] {'grp'}, use_global_device_ids=true, to_apply=%region_31.32 | all-reduce | flops 2048 | bytes 16384 | tf_op jit(solution)/shard_map/psum | solution.py:107
  920.1 62.4 %psum.63 = f32[8]{0:T(128)S(1)} all-reduce(f32[8]{0:T(128)S(1)} %get-tuple-element.34), channel_id=1, replica_groups=mesh['grp'=4,'dev'=32] {'grp','dev'}, use_global_device_ids=true, to_apply=%region_34.35 | all-reduce | flops 8 | bytes 64 | tf_op jit(solution)/shard_map/psum | solution.py:116
  (228 shorter events, 255.1 us)
Async XLA Ops:
  7.2 34.5 %copy-start.3 = (s32[1,4]{1,0:T(1,128)S(1)}, s32[1,4]{1,0:T(1,128)}, u32[]{:S(2)}) copy-start(s32[1,4]{1,0:T(1,128)} %param.5) | copy-start | bytes 52
  7.2 72.4 %all-reduce.6.cloned.1.call-start = ((), (), s32[]{:S(2)}) async-start(), calls=%async_computation.2 | async-start | bytes 720896 | tf_op jit(solution)/shard_map/psum | solution.py:25
  8.6 33.3 %collective-permute-start = (f32[1,11,256]{2,0,1:T(1,128)S(1)}, f32[1,11,256]{2,0,1:T(1,128)S(1)}, u32[]{:S(2)}, u32[]{:S(2)}) collective-permute-start(f32[1,11,256]{2,0,1:T(1,128)S(1)} %constant_dynamic-update-slice_fusion), channel_id=1, source_target_pairs={{0,1},{1,2},{2,3},{3,4},{4,5},{5,6},{6,7},{7,8},{8,9},{9,10},{10,1... | collective-permute-start | bytes 33800 | tf_op jit(solution)/shard_map/ppermute | solution.py:20
  38.0 588.0 %reduce-scatter.3.cloned.1.call-start = ((), (), s32[]{:S(2)}) async-start(), calls=%async_computation.4 | async-start | bytes 270336 | tf_op jit(solution)/shard_map/reduce_scatter | solution.py:108
  119.7 2.7 copy-start
  539.4 97.3 %copy-start.1 = (f32[1,8,256]{2,1,0:T(8,128)S(1)}, f32[1,8,256]{2,1,0:T(8,128)}, u32[]{:S(2)}) copy-start(f32[1,8,256]{2,1,0:T(8,128)} %param.6) | copy-start | bytes 24580
  539.4 97.3 %copy-start.2 = (f32[1,8,256]{2,1,0:T(8,128)S(1)}, f32[1,8,256]{2,1,0:T(8,128)}, u32[]{:S(2)}) copy-start(f32[1,8,256]{2,1,0:T(8,128)} %param.7) | copy-start | bytes 24580
  547.8 279.0 %all-reduce.8.cloned.1.call-start = ((), (), s32[]{:S(2)}) async-start(), calls=%async_computation.3 | async-start | bytes 524288 | tf_op jit(solution)/shard_map/psum | solution.py:25
  548.2 88.5 %collective-permute-start.1 = (f32[1,8,256]{2,1,0:T(8,128)S(1)}, f32[1,8,256]{2,1,0:T(8,128)S(1)}, u32[]{:S(2)}, u32[]{:S(2)}) collective-permute-start(f32[1,8,256]{2,1,0:T(8,128)S(1)} %copy.84), channel_id=1, source_target_pairs={{1,0},{2,1},{3,2},{4,3},{5,4},{6,5},{7,6},{8,7},{9,8},{10,9},{11,1... | collective-permute-start | bytes 24584 | tf_op jit(solution)/shard_map/ppermute | solution.py:20
  786.9 122.4 %reduce-scatter.5.cloned.1.call-start = ((), (), s32[]{:S(2)}) async-start(), calls=%async_computation.5 | async-start | bytes 270336 | tf_op jit(solution)/shard_map/reduce_scatter | solution.py:108
  786.9 3.1 collective-permute-start.2
  831.5 88.5 %collective-permute-start.3 = (f32[1,8,256]{2,1,0:T(8,128)S(1)}, f32[1,8,256]{2,1,0:T(8,128)S(1)}, u32[]{:S(2)}, u32[]{:S(2)}) collective-permute-start(f32[1,8,256]{2,1,0:T(8,128)S(1)} %copy.88), channel_id=1, source_target_pairs={{1,0},{2,1},{3,2},{4,3},{5,4},{6,5},{7,6},{8,7},{9,8},{10,9},{11,1... | collective-permute-start | bytes 24584 | tf_op jit(solution)/shard_map/ppermute | solution.py:20
Sparse Core Ops, SparseCore 0:
  38.1 41.3 all-reduce.5
  547.9 78.0 reduce-scatter.2
  787.0 39.7 all-reduce.7
  831.2 78.0 reduce-scatter.4
where the time goes:
time: 1000 us; the launch traced here: 990 us
  other arithmetic  353 us (35%)
  blocking collectives  260 us (26%)
  waiting for transfers between devices  228 us (23%)
  matrix products  61.2 us (6%)
  local copies, waits for them, and re-layouts  60.9 us (6%)
  between operations  21.3 us (2%)
    another operation x38, other arithmetic, kernel_factor(): factor_lower = jnp.linalg.cholesky(covariance)  218 us
    reduce_scatter x2, waiting for transfers between devices, local(): lax.psum_scatter(summed_rows, 'dev', scatter_dimension=0, tiled=True)  153 us
    psum x2, blocking collectives, squared_norm(): return lax.psum(jnp.sum(field * field, axis=(0, 2)), ('grp', 'dev'))  127 us
    another operation x3, other arithmetic, kernel_factor(): lax.linalg.triangular_solve(factor_lower, unit_tail, left_side=True, lowe...  105 us
    psum x2, waiting for transfers between devices, from_root(): return lax.psum(kept, axis)  73.8 us
    psum x1, blocking collectives, local(): product = lax.psum(jnp.sum(direction * image, axis=(0, 2)), ('grp', 'dev'))  62.4 us
    all_gather x2, blocking collectives, fetch(): column_rows = lax.all_gather(packed, 'dev', axis=0, tiled=True)  49.4 us
    another operation x18, matrix products, kernel_factor(): factor_lower = jnp.linalg.cholesky(covariance)  34.9 us
  transfers between devices with their start and end apart: 8, of which 5 were waited for; matrix products, arithmetic and copies ran while one was open for 1% of the time, Pallas kernels for 0%

commit v1 on v0

v1 whole, which is shorter than its diff:
```python
import math

import jax
import jax.numpy as jnp
import numpy as np
from jax import lax
from jax.experimental import pallas as pl
from jax.experimental.pallas import tpu as pltpu
from jax.sharding import PartitionSpec as P

SCALE_LENGTH = 0.5
NUGGET = 0.5
SQRT_THREE = math.sqrt(3.0)
F32 = jnp.float32
BF16 = jnp.bfloat16
NN = (((1,), (0,)), ((), ()))
NT = (((1,), (1,)), ((), ()))
DOUBLINGS = 7
GRP, DEV = 4, 32


def coefficients(size):
    low, high = NUGGET, size + NUGGET
    tau = (high + low) / (high - low)
    rows = []
    for _ in range(DOUBLINGS):
        twice = 2.0 * tau * tau - 1.0
        rows.append((2.0 * tau * tau / twice, 1.0 / twice))
        tau = twice
    return np.array(rows, np.float32), 2.0 / (high + low)


def split(x):
    high = x.astype(BF16)
    return high, (x - high.astype(F32)).astype(BF16)


def dot(a, b, dims=NN):
    return lax.dot_general(a, b, dims, preferred_element_type=F32)


def dot3(a, b, dims=NN):
    return dot(a[0], b[0], dims) + (dot(a[0], b[1], dims) + dot(a[1], b[0], dims))


def dot6(a, b, dims=NN):
    return lax.dot_general(
        a, b, dims, preferred_element_type=F32, precision=lax.Precision.HIGHEST
    )


def neighbourhood():
    g, d = lax.axis_index("grp"), lax.axis_index("dev")
    flat = g * DEV + d
    after, before = lax.rem(flat + 1, GRP * DEV), lax.rem(flat + GRP * DEV - 1, GRP * DEV)
    return g, d, place(after), place(before)


def place(flat):
    return {"grp": flat // DEV, "dev": lax.rem(flat, DEV)}


def greet(g, d, after, before):
    barrier = pltpu.get_barrier_semaphore()

    def one(k, carry):
        pl.semaphore_signal(
            barrier, 1, device_id={"grp": g, "dev": lax.rem(d + k, DEV)}
        )
        return carry

    lax.fori_loop(1, DEV, one, 0)
    for k in range(1, GRP):
        pl.semaphore_signal(barrier, 1, device_id={"grp": lax.rem(g + k, GRP), "dev": d})
    pl.semaphore_signal(barrier, 1, device_id=after)
    pl.semaphore_signal(barrier, 1, device_id=before)
    return barrier


def remote(src, dst, send, recv, device):
    return pltpu.make_async_remote_copy(
        src_ref=src, dst_ref=dst, send_sem=send, recv_sem=recv, device_id=device
    )


def gather_kernel(
    loc, obs, prev_loc, prev_obs, col_obs, all_loc, all_obs, col_loc, sems_s, sems_r, sem_l
):
    g, d, after, before = neighbourhood()
    barrier = greet(g, d, after, before)
    pl.semaphore_wait(barrier, DEV - 1 + GRP - 1 + 2)
    ahead = [
        remote(loc.at[0], prev_loc, sems_s.at[0], sems_r.at[0], after),
        remote(obs.at[0], prev_obs, sems_s.at[1], sems_r.at[1], after),
    ]
    column = []
    for k in range(1, GRP):
        mate = {"grp": k, "dev": d}
        column.append(remote(loc.at[0], col_loc, sems_s.at[2 * k], sems_r.at[2], mate))
        column.append(remote(obs.at[0], col_obs, sems_s.at[2 * k + 1], sems_r.at[3], mate))
    own = [
        pltpu.make_async_copy(loc.at[0], col_loc, sem_l.at[0]),
        pltpu.make_async_copy(obs.at[0], col_obs, sem_l.at[1]),
    ]

    @pl.when(g == 0)
    def _():
        for c in column + own:
            c.start()

    for c in ahead:
        c.start()

    @pl.when(g == 0)
    def _():
        for c in own:
            c.wait()

    @pl.when(g != 0)
    def _():
        column[0].wait_recv()
        column[1].wait_recv()

    mine = [
        pltpu.make_async_copy(col_loc, all_loc.at[d], sem_l.at[0]),
        pltpu.make_async_copy(col_obs, all_obs.at[d], sem_l.at[1]),
    ]
    for c in mine:
        c.start()

    def spread(k, carry):
        peer = {"grp": g, "dev": lax.rem(d + k, DEV)}
        remote(col_loc, all_loc.at[d], sems_s.at[8], sems_r.at[4], peer).start()
        remote(col_obs, all_obs.at[d], sems_s.at[9], sems_r.at[5], peer).start()
        return carry

    lax.fori_loop(1, DEV, spread, 0)
    others = pl.ds(0, DEV - 1)
    for whole, s, r in ((all_loc, 8, 4), (all_obs, 9, 5)):
        piece = whole.at[others]
        c = remote(piece, piece, sems_s.at[s], sems_r.at[r], after)
        c.wait_send()
        c.wait_recv()
    for c in mine + ahead:
        c.wait()

    @pl.when(g == 0)
    def _():
        for c in column:
            c.wait_send()


def factor_kernel(near, coef, prev_loc, all_loc, loc, g_out, p_out, tiles, low, r_ref, x_ref):
    size = loc.shape[2]
    first = coefficients(size)[1]
    live = [jnp.where(near[0, s] >= 0, 1.0, 0.0).astype(F32) for s in (0, 2, 3)] + [1.0]
    points = [
        prev_loc[...],
        all_loc[jnp.maximum(near[0, 2], 0)],
        all_loc[jnp.maximum(near[0, 3], 0)],
        loc[0],
    ]
    rows = lax.broadcasted_iota(jnp.int32, (size, size), 0)
    columns = lax.broadcasted_iota(jnp.int32, (size, size), 1)
    eye = (rows == columns).astype(F32)
    for i in range(4):
        padded = jnp.concatenate([points[i], jnp.zeros((5, size), F32)], axis=0)
        upright = padded.T
        for j in range(i + 1):
            total = None
            for c in range(3):
                offset = upright[:, c : c + 1] - points[j][c : c + 1, :]
                total = offset * offset if total is None else total + offset * offset
            scaled = (SQRT_THREE / SCALE_LENGTH) * jnp.sqrt(total)
            value = (1.0 + scaled) * jnp.exp(-scaled) * (live[i] * live[j])
            if i == j:
                value = value + eye * (NUGGET * live[i] + (1.0 - live[i]))
            tiles[i, j] = value

    def inverse(k):
        matrix = tiles[k, k]
        r = eye - first * matrix
        x_ref[...] = (first * coef[0, 0]) * (eye + r)
        pair = split(r)
        r_ref[...] = coef[0, 0] * dot3(pair, pair) - coef[0, 1] * eye

        def body(n, carry):
            pair = split(r_ref[...])
            x = x_ref[...]
            a, c = coef[n, 0], coef[n, 1]
            moved = dot3(split(x), pair)
            square = dot3(pair, pair)
            x_ref[...] = a * (x + moved)
            r_ref[...] = a * square - c * eye
            return carry

        lax.fori_loop(1, DOUBLINGS, body, 0)
        x = x_ref[...]
        left = eye - dot6(tiles[k, k], x)
        return x + dot3(split(x), split(left))

    for k in range(3):
        inv = inverse(k)
        for i in range(k + 1, 4):
            low[i, k] = dot6(tiles[i, k], inv)
        for j in range(k + 1, 4):
            for i in range(j, 4):
                tiles[i, j] = tiles[i, j] - dot6(low[i, k], tiles[j, k], NT)
    inv = inverse(3)
    p_out[0], p_out[1] = split(inv)
    g2 = -low[3, 2]
    g1 = -(low[3, 1] + dot6(g2, low[2, 1]))
    g0 = -(low[3, 0] + dot6(g1, low[1, 0]) + dot6(g2, low[2, 0]))
    for k, value in enumerate((g0, g1, g2)):
        high, rest = split(value)
        g_out[0, :, k * size : (k + 1) * size] = high
        g_out[1, :, k * size : (k + 1) * size] = rest


def lane_group(shape):
    return lax.broadcasted_iota(jnp.int32, shape, 1) // 32


def pack(parts):
    out = None
    for k, part in enumerate(parts):
        half = part[:, :128] + part[:, 128:] if part.shape[1] == 256 else part
        if half is not part:
            half = half + pltpu.roll(half, 64, 1)
            half = half + pltpu.roll(half, 32, 1)
        group = lane_group(half.shape)
        out = half if out is None else jnp.where(group == k, half, out)
    return out


def unpack(packed, k):
    return jnp.sum(
        jnp.where(lane_group(packed.shape) == k, packed, 0.0), axis=1, keepdims=True
    )


def solve_kernel(
    near, obs, noise, g_mat, p_mat, prev_obs, col_obs, all_obs,
    sol_out, res_out,
    msg, rs1, rs2, x1, x2, back1, back2, hop, ag, rcol, prev1, stage, sems_s, sems_r,
):
    size = obs.shape[2]
    g, d, after, before = neighbourhood()
    barrier = greet(g, d, after, before)
    first_group = jnp.where(g == 0, 1.0, 0.0).astype(F32)
    wi, wj = near[0, 2], near[0, 3]
    b = obs[0]
    prec = noise[0]
    others = pl.ds(0, DEV - 1)

    def dot_small(rows, mat, dims):
        high, rest = split(rows)
        return dot(high, mat[0], dims) + (dot(high, mat[1], dims) + dot(rest, mat[0], dims))

    def apply(own, before_rows, table):
        slots = jnp.concatenate(
            [before_rows, table[jnp.maximum(wi, 0)], table[jnp.maximum(wj, 0)]], axis=1
        )
        v = own + dot_small(slots, g_mat, NT)
        w = dot_small(v, p_mat, NN)
        return v, w, dot_small(w, g_mat, NN)

    def scatter(u, packed, recv, back, k):
        hop[k] = u[:, :size]
        ui, uj = u[:, size : 2 * size], u[:, 2 * size :]

        def fill(m, carry):
            fi = jnp.where(wi == m, 1.0, 0.0).astype(F32)
            fj = jnp.where(wj == m, 1.0, 0.0).astype(F32)
            msg[k, m, :, :size] = fi * ui + fj * uj
            msg[k, m, :, size:] = packed
            return carry

        lax.fori_loop(0, DEV, fill, 0)
        if k == 0:
            pl.semaphore_wait(barrier, DEV - 1 + GRP - 1 + 2)
        returned = remote(hop.at[k], back, sems_s.at[0], sems_r.at[k], before)
        returned.start()
        mine = pltpu.make_async_copy(msg.at[k, d], recv.at[d], sems_s.at[1])
        mine.start()

        def spread(n, carry):
            m = lax.rem(d + n, DEV)
            remote(
                msg.at[k, m], recv.at[d], sems_s.at[2], sems_r.at[2 + k], {"grp": g, "dev": m}
            ).start()
            return carry

        lax.fori_loop(1, DEV, spread, 0)
        piece = recv.at[others]
        every = remote(piece, piece, sems_s.at[2], sems_r.at[2 + k], after)
        every.wait_recv()
        mine.wait()
        returned.wait()
        total = recv[0]
        for n in range(1, DEV):
            total = total + recv[n]
        every.wait_send()
        return total, back[...]

    def across(value, recv, k):
        recv[g] = value
        stage[k] = value
        src = stage.at[k]
        copies = [
            remote(
                src, recv.at[g], sems_s.at[2 + n + 3 * k], sems_r.at[3 + n + 3 * k],
                {"grp": lax.rem(g + n, GRP), "dev": d},
            )
            for n in range(1, GRP)
        ]
        for c in copies:
            c.start()

        for c in copies:
            c.wait()
        return (recv[0] + recv[1]) + (recv[2] + recv[3])

    v0, w0, u0 = apply(b, prev_obs[...], all_obs)
    kept = prec * b
    packed = pack([b * b, v0 * w0 + kept * b])
    total, returned = scatter(u0, packed, rs1, back1, 0)
    own = w0 + kept + returned
    total = jnp.concatenate([total[:, :size] + first_group * own, total[:, size:]], axis=1)
    total = across(total, x1, 0)
    column = total[:, :size]
    rr0, p0 = unpack(total[:, size:], 0), unpack(total[:, size:], 1)
    alpha0 = rr0 / p0
    image0 = jnp.where(g == 0, column, own)
    r1 = b - alpha0 * image0
    rcol[0] = r1
    rcol[1] = col_obs[...] - alpha0 * column
    ahead = remote(rcol.at[0], prev1, sems_s.at[0], sems_r.at[10], after)
    ahead.start()
    mine = pltpu.make_async_copy(rcol.at[1], ag.at[d], sems_s.at[1])
    mine.start()

    def spread(n, carry):
        peer = {"grp": g, "dev": lax.rem(d + n, DEV)}
        remote(rcol.at[1], ag.at[d], sems_s.at[2], sems_r.at[11], peer).start()
        return carry

    lax.fori_loop(1, DEV, spread, 0)
    piece = ag.at[others]
    every = remote(piece, piece, sems_s.at[2], sems_r.at[11], after)
    ahead.wait()
    mine.wait()
    every.wait()
    v1, w1, u1 = apply(r1, prev1[...], ag)
    kept = prec * r1
    packed = pack([v1 * w1 + kept * r1, v1 * w0 + kept * b, r1 * r1])
    total, returned = scatter(u1, packed, rs2, back2, 1)
    own = w1 + kept + returned
    total = jnp.concatenate([total[:, :size] + first_group * own, total[:, size:]], axis=1)
    total = across(total, x2, 1)
    s1, s2, rr1 = (unpack(total[:, size:], k) for k in range(3))
    beta = rr1 / rr0
    alpha1 = rr1 / (s1 + 2.0 * beta * s2 + beta * beta * p0)
    image1 = jnp.where(g == 0, total[:, :size], own) + beta * image0
    sol_out[0] = alpha0 * b + alpha1 * (r1 + beta * b)
    res_out[0] = r1 - alpha1 * image1


def local(locations, neighbours, observations, noise_prec):
    points, fields = locations.shape[2], observations.shape[1]
    vmem = pl.BlockSpec(memory_space=pltpu.VMEM)
    smem = pl.BlockSpec(memory_space=pltpu.SMEM)
    shape = jax.ShapeDtypeStruct
    prev_loc, prev_obs, col_obs, all_loc, all_obs = pl.pallas_call(
        gather_kernel,
        out_shape=(
            shape((3, points), F32),
            shape((fields, points), F32),
            shape((fields, points), F32),
            shape((DEV, 3, points), F32),
            shape((DEV, fields, points), F32),
        ),
        in_specs=[vmem] * 2,
        out_specs=(vmem,) * 5,
        scratch_shapes=[
            pltpu.VMEM((3, points), F32),
            pltpu.SemaphoreType.DMA((10,)),
            pltpu.SemaphoreType.DMA((6,)),
            pltpu.SemaphoreType.DMA((2,)),
        ],
        compiler_params=pltpu.CompilerParams(collective_id=0, has_side_effects=True),
    )(locations, observations)
    g_mat, p_mat = pl.pallas_call(
        factor_kernel,
        out_shape=(shape((2, points, 3 * points), BF16), shape((2, points, points), BF16)),
        in_specs=[smem, smem, vmem, vmem, vmem],
        out_specs=(vmem,) * 2,
        scratch_shapes=[
            pltpu.VMEM((4, 4, points, points), F32),
            pltpu.VMEM((4, 3, points, points), F32),
            pltpu.VMEM((points, points), F32),
            pltpu.VMEM((points, points), F32),
        ],
        compiler_params=pltpu.CompilerParams(vmem_limit_bytes=40 << 20),
    )(neighbours, jnp.asarray(coefficients(points)[0]), prev_loc, all_loc, locations)
    wide = points + 128
    return pl.pallas_call(
        solve_kernel,
        out_shape=(shape((1, fields, points), F32),) * 2,
        in_specs=[smem] + [vmem] * 7,
        out_specs=(vmem,) * 2,
        scratch_shapes=[
            pltpu.VMEM((2, DEV, fields, wide), F32),
            pltpu.VMEM((DEV, fields, wide), F32),
            pltpu.VMEM((DEV, fields, wide), F32),
            pltpu.VMEM((GRP, fields, wide), F32),
            pltpu.VMEM((GRP, fields, wide), F32),
            pltpu.VMEM((fields, points), F32),
            pltpu.VMEM((fields, points), F32),
            pltpu.VMEM((2, fields, points), F32),
            pltpu.VMEM((DEV, fields, points), F32),
            pltpu.VMEM((2, fields, points), F32),
            pltpu.VMEM((fields, points), F32),
            pltpu.VMEM((2, fields, wide), F32),
            pltpu.SemaphoreType.DMA((9,)),
            pltpu.SemaphoreType.DMA((12,)),
        ],
        compiler_params=pltpu.CompilerParams(
            collective_id=1, has_side_effects=True, vmem_limit_bytes=40 << 20
        ),
    )(neighbours, observations, noise_prec, g_mat, p_mat, prev_obs, col_obs, all_obs)


def solution(mesh):
    placed = (
        P(("grp", "dev"), None, None),
        P(("grp", "dev"), None),
        P(("grp", "dev"), None, None),
        P(("grp", "dev"), None, None),
    )
    return jax.shard_map(
        local,
        mesh=mesh,
        in_specs=placed,
        out_specs=(P(("grp", "dev"), None, None), P(("grp", "dev"), None, None)),
        check_vma=False,
    )
```

time: 1000 us -> 81 us (0.08)
  other arithmetic: 353 us -> 0 us
  blocking collectives: 260 us -> 0 us
  waiting for transfers between devices: 228 us -> 0 us
  Pallas kernels: 0 us -> 74.1 us
  matrix products: 61.2 us -> 0 us
  local copies, waits for them, and re-layouts: 60.9 us -> 5.7 us
  between operations: 21.3 us -> 0.72 us
    another operation x41 -> x0, other arithmetic: 324 us -> none  [the longest x38 218 us: kernel_factor(): factor_lower = jnp.linalg.cholesky(covariance)]
    psum x5 -> x0, blocking collectives: 210 us -> none  [the longest x2 127 us: squared_norm(): return lax.psum(jnp.sum(field * field, axis=(0, 2)), ('grp', 'dev'))]
    reduce_scatter x2 -> x0, waiting for transfers between devices: 153 us -> none  [local(): lax.psum_scatter(summed_rows, 'dev', scatter_dimension=0, tiled=True)]
    pallas_call x0 -> x3, Pallas kernels: none -> 74.1 us  [the longest x1 36.5 us: local(): pl.pallas_call(solve_kernel, out_shape=(shape((1, fields, points), F32),)...]
    psum x2 -> x0, waiting for transfers between devices: 73.8 us -> none  [from_root(): return lax.psum(kept, axis)]
    another operation x37 -> x0, matrix products: 53.2 us -> none  [the longest x18 34.9 us: kernel_factor(): factor_lower = jnp.linalg.cholesky(covariance)]
    all_gather x2 -> x0, blocking collectives: 49.4 us -> none  [fetch(): column_rows = lax.all_gather(packed, 'dev', axis=0, tiled=True)]
    another operation x47 -> x0, local copies, waits for them, and re-layouts: 38.1 us -> none
  transfers between devices with their start and end apart: 8 -> 0, of which waited for: 5 -> 0; matrix products, arithmetic and copies ran while one was open for 1% -> 0% of each run, Pallas kernels for 0% -> 0%
where the time goes in v1:
time: 81 us; the launch traced here: 80.5 us
  Pallas kernels  74.1 us (91%)
  local copies, waits for them, and re-layouts  5.7 us (7%)
    pallas_call x1, Pallas kernels, local(): pl.pallas_call(solve_kernel, out_shape=(shape((1, fields, points), F32),)...  36.5 us
    pallas_call x1, Pallas kernels, local(): pl.pallas_call(factor_kernel, out_shape=(shape((2, points, 3 * points), B...  21.9 us
    pallas_call x1, Pallas kernels, local(): pl.pallas_call(gather_kernel, out_shape=(shape((3, points), F32), shape((...  15.7 us
    unnamed x23, local copies, waits for them, and re-layouts  5.7 us

profile of v1, /device:TPU:0, one launch (start us, length us, event | category | flops | bytes accessed | tf_op | source)
XLA Modules:
  0.0 80.5 jit_solution(9759938819419816670)
XLA Ops:
  0.6 1.3 %copy.7.loc = f32[1,3,256]{2,1,0:T(4,128)} copy(f32[1,3,256]{2,0,1:T(1,128)} %param.5) | data formatting | bytes 6144 | tf_op args[0]
  1.9 15.7 %shard_map.68 = (f32[3,256]{1,0:T(4,128)}, f32[8,256]{1,0:T(8,128)}, f32[8,256]{1,0:T(8,128)}, f32[32,3,256]{2,1,0:T(4,128)}, f32[32,8,256]{2,1,0:T(8,128)}) custom-call(f32[1,3,256]{2,1,0:T(4,128)} %copy.7.loc, f32[1,8,256]{2,1,0:T(8,128)} %obs.3), custom_call_target="tpu_custom_call" | custom-call | tf_op jit(solution)/shard_map/pallas_call | solution.py:374
  17.6 0.0 copy-start.7
  17.6 0.0 copy-start.2
  17.6 0.0 copy-start.9
  17.6 0.7 copy-done.7
  18.3 0.0 copy-done.2
  18.3 0.0 copy-done.9
  18.3 0.0 copy-start.1
  18.3 0.9 %copy-done.1 = f32[32,3,256]{2,1,0:T(4,128)S(1)} copy-done((f32[32,3,256]{2,1,0:T(4,128)S(1)}, f32[32,3,256]{2,1,0:T(4,128)}, u32[]{:S(2)}) %copy-start.1) | copy-done | bytes 98328
  19.2 0.0 copy-start.8
  19.2 0.7 copy-done.8
  19.9 0.0 copy-start.3
  19.9 0.0 copy-start.4
  19.9 21.9 %shard_map.69 = (bf16[2,256,768]{2,1,0:T(8,128)(2,1)S(1)}, bf16[2,256,256]{2,1,0:T(8,128)(2,1)S(1)}) custom-call(s32[1,4]{1,0:T(1,128)S(1)} %copy-done.9, f32[7,2]{1,0:T(8,128)S(1)} %copy-done.7, f32[3,256]{1,0:T(4,128)S(1)} %copy-done.8, f32[32,3,256]{2,1,0:T(4,128)S(1)} %copy-done.1, f32[1,3,256]{2,1,0:T(4,128)S(1)} %copy-done.2), custom_call_target="tpu_custom_call" | custom-call | tf_op jit(solution)/shard_map/pallas_call | solution.py:393
  41.8 0.0 copy-done.3
  41.8 0.0 copy-done.4
  41.8 0.0 copy-done.5
  41.8 0.0 copy-done.6
  41.8 0.0 copy-start
  41.8 0.9 %copy-done = f32[32,8,256]{2,1,0:T(8,128)S(1)} copy-done((f32[32,8,256]{2,1,0:T(8,128)S(1)}, f32[32,8,256]{2,1,0:T(8,128)}, u32[]{:S(2)}) %copy-start) | copy-done | bytes 262168
  42.8 36.5 %shard_map.70 = (f32[1,8,256]{2,1,0:T(8,128)S(1)}, f32[1,8,256]{2,1,0:T(8,128)S(1)}) custom-call(s32[1,4]{1,0:T(1,128)S(1)} %copy-done.9, f32[1,8,256]{2,1,0:T(8,128)S(1)} %copy-done.3, f32[1,8,256]{2,1,0:T(8,128)S(1)} %copy-done.4, bf16[2,256,768]{2,1,0:T(8,128)(2,1)S(1)} %get-tuple-element.11.g_mat, bf16[2,256,256]{2,1,0:T(8,128)(2,1)S(1)} %get-tuple-element.12.p_mat, ...), custom_call_target="tpu_custom_call" | custom-call | tf_op jit(solution)/shard_map/pallas_call | solution.py:407
  79.3 0.6 copy.11
  79.9 0.6 copy.12
  (2 shorter events, 0.0 us)
Async XLA Ops:
  17.6 0.7 copy-start.7
  17.6 0.7 copy-start.2
  17.6 0.7 copy-start.9
  18.3 0.9 %copy-start.1 = (f32[32,3,256]{2,1,0:T(4,128)S(1)}, f32[32,3,256]{2,1,0:T(4,128)}, u32[]{:S(2)}) copy-start(f32[32,3,256]{2,1,0:T(4,128)} %get-tuple-element.10.all_loc) | copy-start | bytes 294916
  19.2 0.7 copy-start.8
  19.9 21.9 %copy-start.3 = (f32[1,8,256]{2,1,0:T(8,128)S(1)}, f32[1,8,256]{2,1,0:T(8,128)}, u32[]{:S(2)}) copy-start(f32[1,8,256]{2,1,0:T(8,128)} %obs.3) | copy-start | bytes 24580
  19.9 21.9 %copy-start.4 = (f32[1,8,256]{2,1,0:T(8,128)S(1)}, f32[1,8,256]{2,1,0:T(8,128)}, u32[]{:S(2)}) copy-start(f32[1,8,256]{2,1,0:T(8,128)} %noise.1) | copy-start | bytes 24580
  19.9 21.9 %copy-start.5 = (f32[8,256]{1,0:T(8,128)S(1)}, f32[8,256]{1,0:T(8,128)}, u32[]{:S(2)}) copy-start(f32[8,256]{1,0:T(8,128)} %get-tuple-element.13.prev_obs) | copy-start | bytes 24580
  19.9 21.9 %copy-start.6 = (f32[8,256]{1,0:T(8,128)S(1)}, f32[8,256]{1,0:T(8,128)}, u32[]{:S(2)}) copy-start(f32[8,256]{1,0:T(8,128)} %get-tuple-element.14.col_obs) | copy-start | bytes 24580
  41.8 1.0 %copy-start = (f32[32,8,256]{2,1,0:T(8,128)S(1)}, f32[32,8,256]{2,1,0:T(8,128)}, u32[]{:S(2)}) copy-start(f32[32,8,256]{2,1,0:T(8,128)} %get-tuple-element.15.all_obs) | copy-start | bytes 786436

commit v2 on v1

v2 whole, which is shorter than its diff:
```python
import math

import jax
import jax.numpy as jnp
from jax import lax
from jax.experimental import pallas as pl
from jax.experimental.pallas import tpu as pltpu
from jax.sharding import PartitionSpec as P

SCALE_LENGTH = 0.5
NUGGET = 0.5
SQRT_THREE = math.sqrt(3.0)
F32 = jnp.float32
BF16 = jnp.bfloat16
NN = (((1,), (0,)), ((), ()))
NT = (((1,), (1,)), ((), ()))
DOUBLINGS = 7
GRP, DEV = 4, 32


def coefficients(size):
    low, high = NUGGET, size + NUGGET
    tau = (high + low) / (high - low)
    rows = []
    for _ in range(DOUBLINGS):
        twice = 2.0 * tau * tau - 1.0
        rows.append((2.0 * tau * tau / twice, 1.0 / twice))
        tau = twice
    return rows, 2.0 / (high + low)


def pick(values, n):
    out = jnp.float32(values[-1])
    for k in range(len(values) - 2, -1, -1):
        out = jnp.where(n == k, jnp.float32(values[k]), out)
    return out


def split(x):
    high = x.astype(BF16)
    return high, (x - high.astype(F32)).astype(BF16)


def dot(a, b, dims=NN):
    return lax.dot_general(a, b, dims, preferred_element_type=F32)


def dot3(a, b, dims=NN):
    return dot(a[0], b[0], dims) + (dot(a[0], b[1], dims) + dot(a[1], b[0], dims))


def dot6(a, b, dims=NN):
    return lax.dot_general(
        a, b, dims, preferred_element_type=F32, precision=lax.Precision.HIGHEST
    )


def neighbourhood():
    g, d = lax.axis_index("grp"), lax.axis_index("dev")
    flat = g * DEV + d
    after, before = lax.rem(flat + 1, GRP * DEV), lax.rem(flat + GRP * DEV - 1, GRP * DEV)
    return g, d, place(after), place(before)


def place(flat):
    return {"grp": flat // DEV, "dev": lax.rem(flat, DEV)}


def greet(g, d, after, before):
    barrier = pltpu.get_barrier_semaphore()

    def one(k, carry):
        pl.semaphore_signal(
            barrier, 1, device_id={"grp": g, "dev": lax.rem(d + k, DEV)}
        )
        return carry

    lax.fori_loop(1, DEV, one, 0)
    for k in range(1, GRP):
        pl.semaphore_signal(barrier, 1, device_id={"grp": lax.rem(g + k, GRP), "dev": d})
    pl.semaphore_signal(barrier, 1, device_id=after)
    pl.semaphore_signal(barrier, 1, device_id=before)
    return barrier


def remote(src, dst, send, recv, device):
    return pltpu.make_async_remote_copy(
        src_ref=src, dst_ref=dst, send_sem=send, recv_sem=recv, device_id=device
    )


def lane(shape):
    return lax.broadcasted_iota(jnp.int32, shape, 1)


def sublane(shape):
    return lax.broadcasted_iota(jnp.int32, shape, 0)


def to_row(parts):
    fields = parts[0].shape[0]
    spread = jnp.zeros((fields, 128), F32)
    slot = lane(spread.shape) - sublane(spread.shape)
    for k, part in enumerate(parts):
        spread = jnp.where(slot == k * fields, jnp.sum(part, axis=1, keepdims=True), spread)
    return jnp.sum(spread, axis=0, keepdims=True)


def from_row(row, k, fields):
    spread = jnp.broadcast_to(row, (fields, 128))
    slot = lane(spread.shape) - sublane(spread.shape)
    return jnp.sum(jnp.where(slot == k * fields, spread, 0.0), axis=1, keepdims=True)


def kernel(
    near, loc, obs, noise,
    sol_out, res_out,
    loc_v, obs_v, noise_v, prev_loc, prev_obs, col_loc, col_obs, all_loc, all_obs,
    tiles, low, r_ref, x_ref, g_mat, p_mat,
    msg, rs, xs, stage, hop, back, rcol, prev1, ag,
    sem_in, sem_mine, sem_s, sem_r,
):
    fields, size = obs_v.shape
    g, d, after, before = neighbourhood()
    barrier = greet(g, d, after, before)
    incoming = [
        pltpu.make_async_copy(src, dst, sem_in.at[k])
        for k, (src, dst) in enumerate(((loc, loc_v), (obs.at[0], obs_v), (noise.at[0], noise_v)))
    ]
    for c in incoming:
        c.start()
    others = pl.ds(0, DEV - 1)
    eye = (sublane((size, size)) == lane((size, size))).astype(F32)
    rows, first = coefficients(size)
    first_group = jnp.where(g == 0, 1.0, 0.0).astype(F32)
    wi, wj = near[0, 2], near[0, 3]
    live = [jnp.where(near[0, s] >= 0, 1.0, 0.0).astype(F32) for s in (0, 2, 3)] + [1.0]

    def points(value):
        flat = [value[c] for c in range(3)]
        upright = jnp.concatenate(flat + [jnp.zeros((5, size), F32)], axis=0).T
        return flat, upright

    def covariance(i, j):
        total = None
        for c in range(3):
            offset = pts[i][1][:, c : c + 1] - pts[j][0][c]
            total = offset * offset if total is None else total + offset * offset
        scaled = (SQRT_THREE / SCALE_LENGTH) * jnp.sqrt(total)
        value = (1.0 + scaled) * jnp.exp(-scaled) * (live[i] * live[j])
        if i == j:
            value = value + eye * (NUGGET * live[i] + (1.0 - live[i]))
        tiles[i, j] = value

    def spread(src, dst, s, r):
        def one(n, carry):
            peer = {"grp": g, "dev": lax.rem(d + n, DEV)}
            remote(src, dst.at[d], sem_s.at[s], sem_r.at[r], peer).start()
            return carry

        lax.fori_loop(1, DEV, one, 0)
        piece = dst.at[others]
        return remote(piece, piece, sem_s.at[s], sem_r.at[r], after)

    def local_copy(src, dst, k):
        c = pltpu.make_async_copy(src, dst, sem_mine.at[k])
        c.start()
        return c

    incoming[0].wait()
    pts = [None, None, None, points(loc_v)]
    covariance(3, 3)
    pl.semaphore_wait(barrier, DEV - 1 + GRP - 1 + 2)
    ahead_loc = remote(loc_v, prev_loc, sem_s.at[0], sem_r.at[0], after)
    column_loc = [
        remote(loc_v, col_loc, sem_s.at[1 + k], sem_r.at[1], {"grp": k, "dev": d})
        for k in range(1, GRP)
    ]
    own_loc = pltpu.make_async_copy(loc_v, col_loc, sem_mine.at[0])

    @pl.when(g == 0)
    def _():
        for c in column_loc:
            c.start()
        own_loc.start()

    ahead_loc.start()
    incoming[1].wait()
    incoming[2].wait()
    ahead_obs = remote(obs_v, prev_obs, sem_s.at[5], sem_r.at[2], after)
    column_obs = [
        remote(obs_v, col_obs, sem_s.at[5 + k], sem_r.at[3], {"grp": k, "dev": d})
        for k in range(1, GRP)
    ]
    own_obs = pltpu.make_async_copy(obs_v, col_obs, sem_mine.at[1])
    ahead_obs.start()

    @pl.when(g == 0)
    def _():
        for c in column_obs:
            c.start()
        own_obs.start()

    ahead_loc.wait()
    pts[0] = points(prev_loc)
    covariance(0, 0)

    @pl.when(g == 0)
    def _():
        own_loc.wait()

    @pl.when(g != 0)
    def _():
        column_loc[0].wait_recv()

    mine_loc = local_copy(col_loc, all_loc.at[d], 2)
    every_loc = spread(col_loc, all_loc, 9, 4)

    def inverse(k):
        r = eye - first * tiles[k, k]
        x_ref[...] = (first * rows[0][0]) * (eye + r)
        pair = split(r)
        r_ref[...] = rows[0][0] * dot3(pair, pair) - rows[0][1] * eye

        def body(n, carry):
            pair = split(r_ref[...])
            x = x_ref[...]
            a, c = pick([row[0] for row in rows], n), pick([row[1] for row in rows], n)
            moved = dot3(split(x), pair)
            square = dot3(pair, pair)
            x_ref[...] = a * (x + moved)
            r_ref[...] = a * square - c * eye
            return carry

        lax.fori_loop(1, DOUBLINGS, body, 0)
        x = x_ref[...]
        left = eye - dot6(tiles[k, k], x)
        return x + dot3(split(x), split(left))

    inv = inverse(0)
    covariance(3, 0)
    low[3, 0] = dot6(tiles[3, 0], inv)
    tiles[3, 3] = tiles[3, 3] - dot6(low[3, 0], tiles[3, 0], NT)

    @pl.when(g == 0)
    def _():
        own_obs.wait()

    @pl.when(g != 0)
    def _():
        column_obs[0].wait_recv()

    mine_loc.wait()
    every_loc.wait_recv()
    mine_obs = local_copy(col_obs, all_obs.at[d], 3)
    every_obs = spread(col_obs, all_obs, 10, 5)
    pts[1] = points(all_loc[jnp.maximum(wi, 0)])
    pts[2] = points(all_loc[jnp.maximum(wj, 0)])
    for i, j in ((1, 0), (1, 1), (2, 0), (2, 1), (2, 2), (3, 1), (3, 2)):
        covariance(i, j)
    for k in range(3):
        if k:
            inv = inverse(k)
        for i in range(k + 1, 4):
            if (i, k) != (3, 0):
                low[i, k] = dot6(tiles[i, k], inv)
        for j in range(k + 1, 4):
            for i in range(j, 4):
                if (i, j, k) != (3, 3, 0):
                    tiles[i, j] = tiles[i, j] - dot6(low[i, k], tiles[j, k], NT)
    inv = inverse(3)
    p_mat[0], p_mat[1] = split(inv)
    g2 = -low[3, 2]
    g1 = -(low[3, 1] + dot6(g2, low[2, 1]))
    g0 = -(low[3, 0] + dot6(g1, low[1, 0]) + dot6(g2, low[2, 0]))
    for k, value in enumerate((g0, g1, g2)):
        high, rest = split(value)
        g_mat[0, :, k * size : (k + 1) * size] = high
        g_mat[1, :, k * size : (k + 1) * size] = rest

    def dot_small(rows, mat, dims):
        high, rest = split(rows)
        return dot(high, mat[0], dims) + (dot(high, mat[1], dims) + dot(rest, mat[0], dims))

    def apply(own, before_rows, table):
        slots = jnp.concatenate(
            [before_rows, table[jnp.maximum(wi, 0)], table[jnp.maximum(wj, 0)]], axis=1
        )
        v = own + dot_small(slots, g_mat, NT)
        w = dot_small(v, p_mat, NN)
        return v, w, dot_small(w, g_mat, NN)

    def reduce(u, own, row, k):
        hop[k] = u[:, :size]
        half = size // 2
        ui, uj = u[:, size : 2 * size], u[:, 2 * size :]

        def fill(m, carry):
            fi = jnp.where(wi == m, 1.0, 0.0).astype(F32)
            fj = jnp.where(wj == m, 1.0, 0.0).astype(F32)
            block = fi * ui + fj * uj
            msg[k, m, :fields] = block[:, :half]
            msg[k, m, fields : 2 * fields] = block[:, half:]
            msg[k, m, 2 * fields :] = row
            return carry

        lax.fori_loop(0, DEV, fill, 0)
        returned = remote(hop.at[k], back.at[k], sem_s.at[11], sem_r.at[6 + k], before)
        returned.start()
        mine = local_copy(msg.at[k, d], rs.at[k, d], 0)

        def one(n, carry):
            m = lax.rem(d + n, DEV)
            remote(
                msg.at[k, m], rs.at[k, d], sem_s.at[12], sem_r.at[8 + k], {"grp": g, "dev": m}
            ).start()
            return carry

        lax.fori_loop(1, DEV, one, 0)
        piece = rs.at[k, others]
        every = remote(piece, piece, sem_s.at[12], sem_r.at[8 + k], after)
        returned.wait()
        own = own + back[k]
        every.wait_recv()
        mine.wait()
        total = rs[k, 0]
        for n in range(1, DEV):
            total = total + rs[k, n]
        held = first_group * jnp.concatenate(
            [own[:, :half], own[:, half:], jnp.zeros((1, half), F32)], axis=0
        )
        total = total + held
        xs[k, g] = total
        stage[k] = total
        copies = [
            remote(
                stage.at[k], xs.at[k, g], sem_s.at[12 + n], sem_r.at[9 + n + 3 * k],
                {"grp": lax.rem(g + n, GRP), "dev": d},
            )
            for n in range(1, GRP)
        ]
        for c in copies:
            c.start()
        every.wait_send()
        for c in copies:
            c.wait()
        total = (xs[k, 0] + xs[k, 1]) + (xs[k, 2] + xs[k, 3])
        column = jnp.concatenate([total[:fields], total[fields : 2 * fields]], axis=1)
        image = jnp.where(g == 0, column, own)
        return image, column, total[2 * fields :]

    ahead_obs.wait()
    mine_obs.wait()
    every_obs.wait_recv()
    b, prec = obs_v[...], noise_v[...]
    v0, w0, u0 = apply(b, prev_obs[...], all_obs)
    kept = prec * b
    image0, column, row = reduce(u0, w0 + kept, to_row([b * b, v0 * w0 + kept * b]), 0)
    rr0, p0 = from_row(row, 0, fields), from_row(row, 1, fields)
    alpha0 = rr0 / p0
    r1 = b - alpha0 * image0
    rcol[0] = r1
    rcol[1] = col_obs[...] - alpha0 * column
    ahead = remote(rcol.at[0], prev1, sem_s.at[11], sem_r.at[16], after)
    ahead.start()
    mine = local_copy(rcol.at[1], ag.at[d], 0)
    every = spread(rcol.at[1], ag, 12, 17)
    ahead.wait()
    mine.wait()
    every.wait()
    v1, w1, u1 = apply(r1, prev1[...], ag)
    kept = prec * r1
    image1, column, row = reduce(
        u1, w1 + kept, to_row([v1 * w1 + kept * r1, v1 * w0 + kept * b, r1 * r1]), 1
    )
    s1, s2, rr1 = (from_row(row, k, fields) for k in range(3))
    beta = rr1 / rr0
    alpha1 = rr1 / (s1 + 2.0 * beta * s2 + beta * beta * p0)
    image1 = image1 + beta * image0
    sol_out[0] = alpha0 * b + alpha1 * (r1 + beta * b)
    res_out[0] = r1 - alpha1 * image1
    every_loc.wait_send()
    every_obs.wait_send()

    @pl.when(g == 0)
    def _():
        for c in column_loc + column_obs:
            c.wait_send()


def local(locations, neighbours, observations, noise_prec):
    points, fields = locations.shape[2], observations.shape[1]
    vmem = pl.BlockSpec(memory_space=pltpu.VMEM)
    smem = pl.BlockSpec(memory_space=pltpu.SMEM)
    hbm = pl.BlockSpec(memory_space=pltpu.HBM)

    def f32(*shape):
        return pltpu.VMEM(shape, F32)

    tall = 2 * fields + 1
    return pl.pallas_call(
        kernel,
        out_shape=(jax.ShapeDtypeStruct((1, fields, points), F32),) * 2,
        in_specs=[smem, hbm, hbm, hbm],
        out_specs=(vmem,) * 2,
        scratch_shapes=[
            f32(3, 1, points), f32(fields, points), f32(fields, points),
            f32(3, 1, points), f32(fields, points),
            f32(3, 1, points), f32(fields, points),
            f32(DEV, 3, 1, points), f32(DEV, fields, points),
            f32(4, 4, points, points), f32(4, 3, points, points),
            f32(points, points), f32(points, points),
            pltpu.VMEM((2, points, 3 * points), BF16), pltpu.VMEM((2, points, points), BF16),
            f32(2, DEV, tall, points // 2), f32(2, DEV, tall, points // 2),
            f32(2, GRP, tall, points // 2), f32(2, tall, points // 2),
            f32(2, fields, points), f32(2, fields, points),
            f32(2, fields, points), f32(fields, points), f32(DEV, fields, points),
            pltpu.SemaphoreType.DMA((3,)),
            pltpu.SemaphoreType.DMA((4,)),
            pltpu.SemaphoreType.DMA((16,)),
            pltpu.SemaphoreType.DMA((18,)),
        ],
        compiler_params=pltpu.CompilerParams(
            collective_id=0, has_side_effects=True, vmem_limit_bytes=48 << 20
        ),
    )(neighbours, jnp.transpose(locations, (1, 0, 2)), observations, noise_prec)


def solution(mesh):
    placed = (
        P(("grp", "dev"), None, None),
        P(("grp", "dev"), None),
        P(("grp", "dev"), None, None),
        P(("grp", "dev"), None, None),
    )
    return jax.shard_map(
        local,
        mesh=mesh,
        in_specs=placed,
        out_specs=(P(("grp", "dev"), None, None), P(("grp", "dev"), None, None)),
        check_vma=False,
    )
```

time: 81 us -> 67.4 us (0.83)
  Pallas kernels: 74.1 us -> 62.5 us
  local copies, waits for them, and re-layouts: 5.7 us -> 3.92 us
    pallas_call x3 -> x1, Pallas kernels: 74.1 us -> 62.5 us  [local(): pl.pallas_call(kernel, out_shape=(jax.ShapeDtypeStruct((1, fields, points...]
    unnamed x23 -> x10, local copies, waits for them, and re-layouts: 5.7 us -> 3.92 us
where the time goes in v2:
time: 67.4 us; the launch traced here: 67 us
  Pallas kernels  62.5 us (93%)
  local copies, waits for them, and re-layouts  3.92 us (6%)
    pallas_call x1, Pallas kernels, local(): pl.pallas_call(kernel, out_shape=(jax.ShapeDtypeStruct((1, fields, points...  62.5 us
    unnamed x10, local copies, waits for them, and re-layouts  3.92 us

profile of v2, /device:TPU:0, one launch (start us, length us, event | category | flops | bytes accessed | tf_op | source)
XLA Modules:
  0.0 67.0 jit_solution(2532880174492135142)
XLA Ops:
  0.6 0.0 copy-start.3
  0.6 0.6 copy-done.3
  1.3 0.0 copy-start
  1.3 0.7 %copy-done = f32[1,8,256]{2,1,0:T(8,128)S(1)} copy-done((f32[1,8,256]{2,1,0:T(8,128)S(1)}, f32[1,8,256]{2,1,0:T(8,128)}, u32[]{:S(2)}) %copy-start) | copy-done | bytes 8216
  2.0 0.0 copy-start.1
  2.0 0.7 %copy-done.1 = f32[1,8,256]{2,1,0:T(8,128)S(1)} copy-done((f32[1,8,256]{2,1,0:T(8,128)S(1)}, f32[1,8,256]{2,1,0:T(8,128)}, u32[]{:S(2)}) %copy-start.1) | copy-done | bytes 8216
  2.7 0.0 copy-start.2
  2.7 0.7 %copy-done.2 = f32[1,3,256]{2,0,1:T(1,128)S(1)} copy-done((f32[1,3,256]{2,0,1:T(1,128)S(1)}, f32[1,3,256]{2,0,1:T(1,128)}, u32[]{:S(2)}) %copy-start.2) | copy-done | bytes 3096
  3.4 62.5 %shard_map.59 = (f32[1,8,256]{2,1,0:T(8,128)S(1)}, f32[1,8,256]{2,1,0:T(8,128)S(1)}) custom-call(s32[1,4]{1,0:T(1,128)S(1)} %copy-done.3, f32[3,1,256]{2,1,0:T(1,128)S(1)} %bitcast.1, f32[1,8,256]{2,1,0:T(8,128)S(1)} %copy-done, f32[1,8,256]{2,1,0:T(8,128)S(1)} %copy-done.1), custom_call_target="tpu_custom_call" | custom-call | tf_op jit(solution)/shard_map/pallas_call | solution.py:401
  65.8 0.6 copy.8
  66.4 0.6 copy.9
Async XLA Ops:
  0.6 0.7 copy-start.3
  1.3 0.7 %copy-start = (f32[1,8,256]{2,1,0:T(8,128)S(1)}, f32[1,8,256]{2,1,0:T(8,128)}, u32[]{:S(2)}) copy-start(f32[1,8,256]{2,1,0:T(8,128)} %obs.1) | copy-start | bytes 24580
  2.0 0.7 %copy-start.1 = (f32[1,8,256]{2,1,0:T(8,128)S(1)}, f32[1,8,256]{2,1,0:T(8,128)}, u32[]{:S(2)}) copy-start(f32[1,8,256]{2,1,0:T(8,128)} %noise.1) | copy-start | bytes 24580
  2.7 0.7 %copy-start.2 = (f32[1,3,256]{2,0,1:T(1,128)S(1)}, f32[1,3,256]{2,0,1:T(1,128)}, u32[]{:S(2)}) copy-start(f32[1,3,256]{2,0,1:T(1,128)} %param.4) | copy-start | bytes 9220

commit v3 on v2

--- a/solution.py
+++ b/solution.py
@@ -62,6 +62,15 @@
     return g, d, place(after), place(before)
 
 
+def mates(d):
+    far = (2, 1, 3, 0)
+    y, z, c = d // 8, lax.rem(d // 2, 4), lax.rem(d, 2)
+    ys = {k: lax.rem(y + k, 4) * 8 for k in far}
+    zs = {k: lax.rem(z + k, 4) * 2 for k in far}
+    cs = {1: 1 - c, 0: c}
+    return [ys[a] + (zs[b] + cs[e]) for a in far for b in far for e in (1, 0)][:-1]
+
+
 def place(flat):
     return {"grp": flat // DEV, "dev": lax.rem(flat, DEV)}
 
@@ -113,9 +122,9 @@
 
 
 def kernel(
-    near, loc, obs, noise,
-    sol_out, res_out,
-    loc_v, obs_v, noise_v, prev_loc, prev_obs, col_loc, col_obs, all_loc, all_obs,
+    near_hbm, loc, obs, noise,
+    out,
+    near, loc_v, obs_v, noise_v, prev_loc, prev_obs, col_loc, col_obs, all_loc, all_obs,
     tiles, low, r_ref, x_ref, g_mat, p_mat,
     msg, rs, xs, stage, hop, back, rcol, prev1, ag,
     sem_in, sem_mine, sem_s, sem_r,
@@ -125,17 +134,17 @@
     barrier = greet(g, d, after, before)
     incoming = [
         pltpu.make_async_copy(src, dst, sem_in.at[k])
-        for k, (src, dst) in enumerate(((loc, loc_v), (obs.at[0], obs_v), (noise.at[0], noise_v)))
+        for k, (src, dst) in enumerate(
+            ((loc, loc_v), (near_hbm, near), (obs.at[0], obs_v), (noise.at[0], noise_v))
+        )
     ]
     for c in incoming:
         c.start()
     others = pl.ds(0, DEV - 1)
+    plane = mates(d)
     eye = (sublane((size, size)) == lane((size, size))).astype(F32)
     rows, first = coefficients(size)
     first_group = jnp.where(g == 0, 1.0, 0.0).astype(F32)
-    wi, wj = near[0, 2], near[0, 3]
-    live = [jnp.where(near[0, s] >= 0, 1.0, 0.0).astype(F32) for s in (0, 2, 3)] + [1.0]
-
     def points(value):
         flat = [value[c] for c in range(3)]
         upright = jnp.concatenate(flat + [jnp.zeros((5, size), F32)], axis=0).T
@@ -153,12 +162,8 @@
         tiles[i, j] = value
 
     def spread(src, dst, s, r):
-        def one(n, carry):
-            peer = {"grp": g, "dev": lax.rem(d + n, DEV)}
-            remote(src, dst.at[d], sem_s.at[s], sem_r.at[r], peer).start()
-            return carry
-
-        lax.fori_loop(1, DEV, one, 0)
+        for m in plane:
+            remote(src, dst.at[d], sem_s.at[s], sem_r.at[r], {"grp": g, "dev": m}).start()
         piece = dst.at[others]
         return remote(piece, piece, sem_s.at[s], sem_r.at[r], after)
 
@@ -168,6 +173,9 @@
         return c
 
     incoming[0].wait()
+    incoming[1].wait()
+    wi, wj = near[0, 2], near[0, 3]
+    live = [jnp.where(near[0, s] >= 0, 1.0, 0.0).astype(F32) for s in (0, 2, 3)] + [1.0]
     pts = [None, None, None, points(loc_v)]
     covariance(3, 3)
     pl.semaphore_wait(barrier, DEV - 1 + GRP - 1 + 2)
@@ -185,8 +193,8 @@
         own_loc.start()
 
     ahead_loc.start()
-    incoming[1].wait()
     incoming[2].wait()
+    incoming[3].wait()
     ahead_obs = remote(obs_v, prev_obs, sem_s.at[5], sem_r.at[2], after)
     column_obs = [
         remote(obs_v, col_obs, sem_s.at[5 + k], sem_r.at[3], {"grp": k, "dev": d})
@@ -309,14 +317,10 @@
         returned.start()
         mine = local_copy(msg.at[k, d], rs.at[k, d], 0)
 
-        def one(n, carry):
-            m = lax.rem(d + n, DEV)
+        for m in plane:
             remote(
                 msg.at[k, m], rs.at[k, d], sem_s.at[12], sem_r.at[8 + k], {"grp": g, "dev": m}
             ).start()
-            return carry
-
-        lax.fori_loop(1, DEV, one, 0)
         piece = rs.at[k, others]
         every = remote(piece, piece, sem_s.at[12], sem_r.at[8 + k], after)
         returned.wait()
@@ -337,7 +341,7 @@
                 stage.at[k], xs.at[k, g], sem_s.at[12 + n], sem_r.at[9 + n + 3 * k],
                 {"grp": lax.rem(g + n, GRP), "dev": d},
             )
-            for n in range(1, GRP)
+            for n in (2, 1, 3)
         ]
         for c in copies:
             c.start()
@@ -377,8 +381,8 @@
     beta = rr1 / rr0
     alpha1 = rr1 / (s1 + 2.0 * beta * s2 + beta * beta * p0)
     image1 = image1 + beta * image0
-    sol_out[0] = alpha0 * b + alpha1 * (r1 + beta * b)
-    res_out[0] = r1 - alpha1 * image1
+    out[0] = alpha0 * b + alpha1 * (r1 + beta * b)
+    out[1] = r1 - alpha1 * image1
     every_loc.wait_send()
     every_obs.wait_send()
 
@@ -391,19 +395,23 @@
 def local(locations, neighbours, observations, noise_prec):
     points, fields = locations.shape[2], observations.shape[1]
     vmem = pl.BlockSpec(memory_space=pltpu.VMEM)
-    smem = pl.BlockSpec(memory_space=pltpu.SMEM)
     hbm = pl.BlockSpec(memory_space=pltpu.HBM)
 
     def f32(*shape):
         return pltpu.VMEM(shape, F32)
 
     tall = 2 * fields + 1
-    return pl.pallas_call(
+    held = [
+        pltpu.with_memory_space_constraint(x, pltpu.HBM)
+        for x in (neighbours, jnp.transpose(locations, (1, 0, 2)), observations, noise_prec)
+    ]
+    both = pl.pallas_call(
         kernel,
-        out_shape=(jax.ShapeDtypeStruct((1, fields, points), F32),) * 2,
-        in_specs=[smem, hbm, hbm, hbm],
-        out_specs=(vmem,) * 2,
+        out_shape=jax.ShapeDtypeStruct((2, fields, points), F32),
+        in_specs=[hbm] * 4,
+        out_specs=vmem,
         scratch_shapes=[
+            pltpu.SMEM((1, neighbours.shape[1]), jnp.int32),
             f32(3, 1, points), f32(fields, points), f32(fields, points),
             f32(3, 1, points), f32(fields, points),
             f32(3, 1, points), f32(fields, points),
@@ -415,7 +423,7 @@
             f32(2, GRP, tall, points // 2), f32(2, tall, points // 2),
             f32(2, fields, points), f32(2, fields, points),
             f32(2, fields, points), f32(fields, points), f32(DEV, fields, points),
-            pltpu.SemaphoreType.DMA((3,)),
+            pltpu.SemaphoreType.DMA((4,)),
             pltpu.SemaphoreType.DMA((4,)),
             pltpu.SemaphoreType.DMA((16,)),
             pltpu.SemaphoreType.DMA((18,)),
@@ -423,7 +431,8 @@
         compiler_params=pltpu.CompilerParams(
             collective_id=0, has_side_effects=True, vmem_limit_bytes=48 << 20
         ),
-    )(neighbours, jnp.transpose(locations, (1, 0, 2)), observations, noise_prec)
+    )(*held)
+    return both[:1], both[1:]
 
 
 def solution(mesh):

time: 67.4 us -> 61.4 us (0.911)
  local copies, waits for them, and re-layouts: 3.92 us -> 0.61 us
  Pallas kernels: 62.5 us -> 60.1 us
    unnamed x10 -> x0, local copies, waits for them, and re-layouts: 3.92 us -> none
    pallas_call x1, Pallas kernels: 62.5 us -> 60.1 us  [local(): pl.pallas_call(kernel, out_shape=jax.ShapeDtypeStruct((2, fields, points)...]
where the time goes in v3:
time: 61.4 us; the launch traced here: 61.3 us
  Pallas kernels  60.1 us (98%)
  between operations  0.64 us (1%)
    pallas_call x1, Pallas kernels, local(): pl.pallas_call(kernel, out_shape=jax.ShapeDtypeStruct((2, fields, points)...  60.1 us

profile of v3, /device:TPU:0, one launch (start us, length us, event | category | flops | bytes accessed | tf_op | source)
XLA Modules:
  0.0 61.3 jit_solution(9780147252871408135)
XLA Ops:
  0.6 60.1 %shard_map.59 = f32[2,8,256]{2,1,0:T(8,128)S(1)} custom-call(s32[1,4]{1,0:T(1,128)} %near_hbm.1, f32[3,1,256]{2,1,0:T(1,128)} %bitcast.1, f32[1,8,256]{2,1,0:T(8,128)} %obs.1, f32[1,8,256]{2,1,0:T(8,128)} %noise.1), custom_call_target="tpu_custom_call" | custom-call | tf_op jit(solution)/shard_map/pallas_call | solution.py:408
  60.7 0.6 fusion

commit v4 on v3

--- a/solution.py
+++ b/solution.py
@@ -14,7 +14,7 @@
 BF16 = jnp.bfloat16
 NN = (((1,), (0,)), ((), ()))
 NT = (((1,), (1,)), ((), ()))
-DOUBLINGS = 7
+DOUBLINGS, FULL = 7, 4
 GRP, DEV = 4, 32
 
 
@@ -125,7 +125,7 @@
     near_hbm, loc, obs, noise,
     out,
     near, loc_v, obs_v, noise_v, prev_loc, prev_obs, col_loc, col_obs, all_loc, all_obs,
-    tiles, low, r_ref, x_ref, g_mat, p_mat,
+    tiles, low, g_mat, p_mat,
     msg, rs, xs, stage, hop, back, rcol, prev1, ag,
     sem_in, sem_mine, sem_s, sem_r,
 ):
@@ -224,26 +224,39 @@
     mine_loc = local_copy(col_loc, all_loc.at[d], 2)
     every_loc = spread(col_loc, all_loc, 9, 4)
 
-    def inverse(k):
+    def inverse(k, jobs=()):
+        jobs = list(jobs)
         r = eye - first * tiles[k, k]
-        x_ref[...] = (first * rows[0][0]) * (eye + r)
+        x = (first * rows[0][0]) * (eye + r)
         pair = split(r)
-        r_ref[...] = rows[0][0] * dot3(pair, pair) - rows[0][1] * eye
-
-        def body(n, carry):
-            pair = split(r_ref[...])
-            x = x_ref[...]
-            a, c = pick([row[0] for row in rows], n), pick([row[1] for row in rows], n)
-            moved = dot3(split(x), pair)
-            square = dot3(pair, pair)
-            x_ref[...] = a * (x + moved)
-            r_ref[...] = a * square - c * eye
-            return carry
-
-        lax.fori_loop(1, DOUBLINGS, body, 0)
-        x = x_ref[...]
+        r = rows[0][0] * dot3(pair, pair) - rows[0][1] * eye
+        for n, (a, c) in enumerate(rows[1:], 1):
+            pair, halves = split(r), split(x)
+            if n < FULL:
+                moved, square = dot3(halves, pair), dot3(pair, pair)
+            else:
+                moved = dot(halves[0], pair[0]) + dot(halves[1], pair[0])
+                square = dot(pair[0], pair[0])
+            if jobs:
+                jobs.pop(0)()
+            x = a * (x + moved)
+            r = a * square - c * eye
         left = eye - dot6(tiles[k, k], x)
-        return x + dot3(split(x), split(left))
+        for job in jobs:
+            job()
+        halves, left = split(x), left.astype(BF16)
+        return x + (dot(halves[0], left) + dot(halves[1], left))
+
+    def lower(i, k, inv):
+        low[i, k] = dot6(tiles[i, k], inv)
+
+    def update(i, j, k):
+        tiles[i, j] = tiles[i, j] - dot6(low[i, k], tiles[j, k], NT)
+
+    def put(k, value):
+        high, rest = split(value)
+        g_mat[0, :, k * size : (k + 1) * size] = high
+        g_mat[1, :, k * size : (k + 1) * size] = rest
 
     inv = inverse(0)
     covariance(3, 0)
@@ -264,27 +277,65 @@
     every_obs = spread(col_obs, all_obs, 10, 5)
     pts[1] = points(all_loc[jnp.maximum(wi, 0)])
     pts[2] = points(all_loc[jnp.maximum(wj, 0)])
-    for i, j in ((1, 0), (1, 1), (2, 0), (2, 1), (2, 2), (3, 1), (3, 2)):
-        covariance(i, j)
-    for k in range(3):
-        if k:
-            inv = inverse(k)
-        for i in range(k + 1, 4):
-            if (i, k) != (3, 0):
-                low[i, k] = dot6(tiles[i, k], inv)
-        for j in range(k + 1, 4):
-            for i in range(j, 4):
-                if (i, j, k) != (3, 3, 0):
-                    tiles[i, j] = tiles[i, j] - dot6(low[i, k], tiles[j, k], NT)
-    inv = inverse(3)
-    p_mat[0], p_mat[1] = split(inv)
-    g2 = -low[3, 2]
-    g1 = -(low[3, 1] + dot6(g2, low[2, 1]))
-    g0 = -(low[3, 0] + dot6(g1, low[1, 0]) + dot6(g2, low[2, 0]))
-    for k, value in enumerate((g0, g1, g2)):
-        high, rest = split(value)
-        g_mat[0, :, k * size : (k + 1) * size] = high
-        g_mat[1, :, k * size : (k + 1) * size] = rest
+    covariance(1, 0)
+    covariance(1, 1)
+    lower(1, 0, inv)
+    update(1, 1, 0)
+
+    def one():
+        covariance(2, 0)
+        lower(2, 0, inv)
+
+    def two():
+        covariance(2, 1)
+        update(2, 1, 0)
+
+    def three():
+        covariance(2, 2)
+        update(2, 2, 0)
+
+    def four():
+        covariance(3, 1)
+        update(3, 1, 0)
+
+    def five():
+        covariance(3, 2)
+        update(3, 2, 0)
+
+    inv1 = inverse(1, (one, two, three, four, five))
+    lower(2, 1, inv1)
+    update(2, 2, 1)
+
+    def six():
+        lower(3, 1, inv1)
+
+    def seven():
+        update(3, 2, 1)
+
+    def eight():
+        update(3, 3, 1)
+
+    def nine():
+        low[2, 0] = dot6(low[2, 1], low[1, 0]) - low[2, 0]
+
+    def ten():
+        low[3, 0] = dot6(low[3, 1], low[1, 0]) - low[3, 0]
+
+    inv2 = inverse(2, (six, seven, eight, nine, ten))
+    lower(3, 2, inv2)
+    update(3, 3, 2)
+
+    def eleven():
+        put(2, -low[3, 2])
+
+    def twelve():
+        put(1, dot6(low[3, 2], low[2, 1]) - low[3, 1])
+
+    def thirteen():
+        put(0, low[3, 0] - dot6(low[3, 2], low[2, 0]))
+
+    inv3 = inverse(3, (eleven, twelve, thirteen))
+    p_mat[0], p_mat[1] = split(inv3)
 
     def dot_small(rows, mat, dims):
         high, rest = split(rows)
@@ -417,7 +468,6 @@
             f32(3, 1, points), f32(fields, points),
             f32(DEV, 3, 1, points), f32(DEV, fields, points),
             f32(4, 4, points, points), f32(4, 3, points, points),
-            f32(points, points), f32(points, points),
             pltpu.VMEM((2, points, 3 * points), BF16), pltpu.VMEM((2, points, points), BF16),
             f32(2, DEV, tall, points // 2), f32(2, DEV, tall, points // 2),
             f32(2, GRP, tall, points // 2), f32(2, tall, points // 2),

time: 61.4 us -> 59.1 us (0.963)
  Pallas kernels: 60.1 us -> 57.7 us
    pallas_call x1, Pallas kernels: 60.1 us -> 57.7 us  [local(): pl.pallas_call(kernel, out_shape=jax.ShapeDtypeStruct((2, fields, points)...]
where the time goes in v4:
time: 59.1 us; the launch traced here: 58.9 us
  Pallas kernels  57.7 us (98%)
  between operations  0.64 us (1%)
  local copies, waits for them, and re-layouts  0.61 us (1%)
    pallas_call x1, Pallas kernels, local(): pl.pallas_call(kernel, out_shape=jax.ShapeDtypeStruct((2, fields, points)...  57.7 us

profile of v4, /device:TPU:0, one launch (start us, length us, event | category | flops | bytes accessed | tf_op | source)
XLA Modules:
  0.0 58.9 jit_solution(4663278338695590943)
XLA Ops:
  0.6 57.7 %shard_map.59 = f32[2,8,256]{2,1,0:T(8,128)S(1)} custom-call(s32[1,4]{1,0:T(1,128)} %near_hbm.1, f32[3,1,256]{2,1,0:T(1,128)} %bitcast.1, f32[1,8,256]{2,1,0:T(8,128)} %obs.1, f32[1,8,256]{2,1,0:T(8,128)} %noise.1), custom_call_target="tpu_custom_call" | custom-call | tf_op jit(solution)/shard_map/pallas_call | solution.py:459
  58.3 0.6 %fusion = (f32[1,8,256]{2,1,0:T(8,128)}, f32[1,8,256]{2,1,0:T(8,128)}) fusion(f32[2,8,256]{2,1,0:T(8,128)S(1)} %shard_map.59), kind=kLoop, calls=%fused_computation | loop fusion | bytes 32768 | tf_op jit(solution)/shard_map/slice | solution.py:485

commit v5 on v4

--- a/solution.py
+++ b/solution.py
@@ -14,7 +14,7 @@
 BF16 = jnp.bfloat16
 NN = (((1,), (0,)), ((), ()))
 NT = (((1,), (1,)), ((), ()))
-DOUBLINGS, FULL = 7, 4
+DOUBLINGS, FULL, LEAD = 7, 4, 6
 GRP, DEV = 4, 32
 
 
@@ -75,20 +75,14 @@
     return {"grp": flat // DEV, "dev": lax.rem(flat, DEV)}
 
 
-def greet(g, d, after, before):
+def greet(g, d, plane, after, before):
     barrier = pltpu.get_barrier_semaphore()
-
-    def one(k, carry):
-        pl.semaphore_signal(
-            barrier, 1, device_id={"grp": g, "dev": lax.rem(d + k, DEV)}
-        )
-        return carry
-
-    lax.fori_loop(1, DEV, one, 0)
-    for k in range(1, GRP):
+    for k in (2, 1, 3):
         pl.semaphore_signal(barrier, 1, device_id={"grp": lax.rem(g + k, GRP), "dev": d})
+    pl.semaphore_signal(barrier, 1, device_id=before)
     pl.semaphore_signal(barrier, 1, device_id=after)
-    pl.semaphore_signal(barrier, 1, device_id=before)
+    for m in plane:
+        pl.semaphore_signal(barrier, 1, device_id={"grp": g, "dev": m})
     return barrier
 
 
@@ -125,13 +119,14 @@
     near_hbm, loc, obs, noise,
     out,
     near, loc_v, obs_v, noise_v, prev_loc, prev_obs, col_loc, col_obs, all_loc, all_obs,
-    tiles, low, g_mat, p_mat,
+    tiles, low, g_mat, p_mat, h_mat, pre,
     msg, rs, xs, stage, hop, back, rcol, prev1, ag,
     sem_in, sem_mine, sem_s, sem_r,
 ):
     fields, size = obs_v.shape
     g, d, after, before = neighbourhood()
-    barrier = greet(g, d, after, before)
+    plane = mates(d)
+    barrier = greet(g, d, plane, after, before)
     incoming = [
         pltpu.make_async_copy(src, dst, sem_in.at[k])
         for k, (src, dst) in enumerate(
@@ -141,7 +136,6 @@
     for c in incoming:
         c.start()
     others = pl.ds(0, DEV - 1)
-    plane = mates(d)
     eye = (sublane((size, size)) == lane((size, size))).astype(F32)
     rows, first = coefficients(size)
     first_group = jnp.where(g == 0, 1.0, 0.0).astype(F32)
@@ -334,53 +328,61 @@
     def thirteen():
         put(0, low[3, 0] - dot6(low[3, 2], low[2, 0]))
 
-    inv3 = inverse(3, (eleven, twelve, thirteen))
-    p_mat[0], p_mat[1] = split(inv3)
-
     def dot_small(rows, mat, dims):
         high, rest = split(rows)
         return dot(high, mat[0], dims) + (dot(high, mat[1], dims) + dot(rest, mat[0], dims))
 
-    def apply(own, before_rows, table):
+    def forward(own, before_rows, table):
         slots = jnp.concatenate(
             [before_rows, table[jnp.maximum(wi, 0)], table[jnp.maximum(wj, 0)]], axis=1
         )
-        v = own + dot_small(slots, g_mat, NT)
-        w = dot_small(v, p_mat, NN)
-        return v, w, dot_small(w, g_mat, NN)
-
-    def reduce(u, own, row, k):
+        return own + dot_small(slots, g_mat, NT)
+
+    def fourteen():
+        pre[...] = forward(obs_v[...], prev_obs[...], all_obs)
+
+    ahead_obs.wait()
+    mine_obs.wait()
+    every_obs.wait_recv()
+    inv3 = inverse(3, (eleven, twelve, thirteen, fourteen))
+    p_mat[0], p_mat[1] = split(inv3)
+
+    def reduce(u, own, row, k, filler):
         hop[k] = u[:, :size]
         half = size // 2
         ui, uj = u[:, size : 2 * size], u[:, 2 * size :]
 
-        def fill(m, carry):
+        def fill(m):
             fi = jnp.where(wi == m, 1.0, 0.0).astype(F32)
             fj = jnp.where(wj == m, 1.0, 0.0).astype(F32)
             block = fi * ui + fj * uj
             msg[k, m, :fields] = block[:, :half]
             msg[k, m, fields : 2 * fields] = block[:, half:]
             msg[k, m, 2 * fields :] = row
-            return carry
-
-        lax.fori_loop(0, DEV, fill, 0)
+
         returned = remote(hop.at[k], back.at[k], sem_s.at[11], sem_r.at[6 + k], before)
+        targets = plane + [d]
+        for m in targets[:LEAD]:
+            fill(m)
         returned.start()
-        mine = local_copy(msg.at[k, d], rs.at[k, d], 0)
-
-        for m in plane:
+        for n, m in enumerate(plane):
+            if n + LEAD < DEV:
+                fill(targets[n + LEAD])
             remote(
                 msg.at[k, m], rs.at[k, d], sem_s.at[12], sem_r.at[8 + k], {"grp": g, "dev": m}
             ).start()
+        mine = local_copy(msg.at[k, d], rs.at[k, d], 0)
+        filler()
         piece = rs.at[k, others]
         every = remote(piece, piece, sem_s.at[12], sem_r.at[8 + k], after)
         returned.wait()
         own = own + back[k]
         every.wait_recv()
         mine.wait()
-        total = rs[k, 0]
-        for n in range(1, DEV):
-            total = total + rs[k, n]
+        sums = [rs[k, n] for n in range(4)]
+        for n in range(4, DEV):
+            sums[n % 4] = sums[n % 4] + rs[k, n]
+        total = (sums[0] + sums[1]) + (sums[2] + sums[3])
         held = first_group * jnp.concatenate(
             [own[:, :half], own[:, half:], jnp.zeros((1, half), F32)], axis=0
         )
@@ -404,13 +406,21 @@
         image = jnp.where(g == 0, column, own)
         return image, column, total[2 * fields :]
 
-    ahead_obs.wait()
-    mine_obs.wait()
-    every_obs.wait_recv()
     b, prec = obs_v[...], noise_v[...]
-    v0, w0, u0 = apply(b, prev_obs[...], all_obs)
+    v0 = pre[...]
+    w0 = dot_small(v0, p_mat, NN)
+    u0 = dot_small(w0, g_mat, NN)
     kept = prec * b
-    image0, column, row = reduce(u0, w0 + kept, to_row([b * b, v0 * w0 + kept * b]), 0)
+
+    def joined():
+        left = (p_mat[0], p_mat[1])
+        for k in range(3):
+            cut = slice(k * size, (k + 1) * size)
+            h_mat[0, :, cut], h_mat[1, :, cut] = split(
+                dot3(left, (g_mat[0, :, cut], g_mat[1, :, cut]))
+            )
+
+    image0, column, row = reduce(u0, w0 + kept, to_row([b * b, v0 * w0 + kept * b]), 0, joined)
     rr0, p0 = from_row(row, 0, fields), from_row(row, 1, fields)
     alpha0 = rr0 / p0
     r1 = b - alpha0 * image0
@@ -423,10 +433,13 @@
     ahead.wait()
     mine.wait()
     every.wait()
-    v1, w1, u1 = apply(r1, prev1[...], ag)
+    v1 = forward(r1, prev1[...], ag)
+    w1 = dot_small(v1, p_mat, NN)
+    u1 = dot_small(v1, h_mat, NN)
     kept = prec * r1
     image1, column, row = reduce(
-        u1, w1 + kept, to_row([v1 * w1 + kept * r1, v1 * w0 + kept * b, r1 * r1]), 1
+        u1, w1 + kept, to_row([v1 * w1 + kept * r1, v1 * w0 + kept * b, r1 * r1]), 1,
+        lambda: None,
     )
     s1, s2, rr1 = (from_row(row, k, fields) for k in range(3))
     beta = rr1 / rr0
@@ -469,6 +482,7 @@
             f32(DEV, 3, 1, points), f32(DEV, fields, points),
             f32(4, 4, points, points), f32(4, 3, points, points),
             pltpu.VMEM((2, points, 3 * points), BF16), pltpu.VMEM((2, points, points), BF16),
+            pltpu.VMEM((2, points, 3 * points), BF16), f32(fields, points),
             f32(2, DEV, tall, points // 2), f32(2, DEV, tall, points // 2),
             f32(2, GRP, tall, points // 2), f32(2, tall, points // 2),
             f32(2, fields, points), f32(2, fields, points),

time: 59.1 us -> 57.7 us (0.976)
  Pallas kernels: 57.7 us -> 56.3 us
    pallas_call x1, Pallas kernels: 57.7 us -> 56.3 us  [local(): pl.pallas_call(kernel, out_shape=jax.ShapeDtypeStruct((2, fields, points)...]
where the time goes in v5:
time: 57.7 us; the launch traced here: 57.5 us
  Pallas kernels  56.3 us (98%)
  between operations  0.64 us (1%)
  local copies, waits for them, and re-layouts  0.61 us (1%)
    pallas_call x1, Pallas kernels, local(): pl.pallas_call(kernel, out_shape=jax.ShapeDtypeStruct((2, fields, points)...  56.3 us

profile of v5, /device:TPU:0, one launch (start us, length us, event | category | flops | bytes accessed | tf_op | source)
XLA Modules:
  0.0 57.5 jit_solution(18124119895786491298)
XLA Ops:
  0.6 56.3 %shard_map.59 = f32[2,8,256]{2,1,0:T(8,128)S(1)} custom-call(s32[1,4]{1,0:T(1,128)} %near_hbm.1, f32[3,1,256]{2,1,0:T(1,128)} %bitcast.1, f32[1,8,256]{2,1,0:T(8,128)} %obs.1, f32[1,8,256]{2,1,0:T(8,128)} %noise.1), custom_call_target="tpu_custom_call" | custom-call | tf_op jit(solution)/shard_map/pallas_call | solution.py:472
  56.9 0.6 %fusion = (f32[1,8,256]{2,1,0:T(8,128)}, f32[1,8,256]{2,1,0:T(8,128)}) fusion(f32[2,8,256]{2,1,0:T(8,128)S(1)} %shard_map.59), kind=kLoop, calls=%fused_computation | loop fusion | bytes 32768 | tf_op jit(solution)/shard_map/slice | solution.py:499

commit v6 on v5

--- a/solution.py
+++ b/solution.py
@@ -166,35 +166,47 @@
         c.start()
         return c
 
+    pl.semaphore_wait(barrier, DEV - 1 + GRP - 1 + 2)
+    ahead_loc = remote(loc, prev_loc, sem_s.at[0], sem_r.at[0], after)
+    column_loc = [
+        remote(loc, col_loc, sem_s.at[1 + k], sem_r.at[1], {"grp": k, "dev": d})
+        for k in range(1, GRP)
+    ]
+    own_loc = pltpu.make_async_copy(loc, col_loc, sem_mine.at[0])
+    ahead_obs = remote(obs.at[0], prev_obs, sem_s.at[5], sem_r.at[2], after)
+    column_obs = [
+        remote(obs.at[0], col_obs, sem_s.at[5 + k], sem_r.at[3], {"grp": k, "dev": d})
+        for k in range(1, GRP)
+    ]
+    own_obs = pltpu.make_async_copy(obs.at[0], col_obs, sem_mine.at[1])
+
+    @pl.when(g == 0)
+    def _():
+        column_loc[1].start()
+        column_loc[0].start()
+        column_loc[2].start()
+        own_loc.start()
+
+    ahead_loc.start()
     incoming[0].wait()
     incoming[1].wait()
     wi, wj = near[0, 2], near[0, 3]
     live = [jnp.where(near[0, s] >= 0, 1.0, 0.0).astype(F32) for s in (0, 2, 3)] + [1.0]
     pts = [None, None, None, points(loc_v)]
     covariance(3, 3)
-    pl.semaphore_wait(barrier, DEV - 1 + GRP - 1 + 2)
-    ahead_loc = remote(loc_v, prev_loc, sem_s.at[0], sem_r.at[0], after)
-    column_loc = [
-        remote(loc_v, col_loc, sem_s.at[1 + k], sem_r.at[1], {"grp": k, "dev": d})
-        for k in range(1, GRP)
-    ]
-    own_loc = pltpu.make_async_copy(loc_v, col_loc, sem_mine.at[0])
-
-    @pl.when(g == 0)
-    def _():
-        for c in column_loc:
-            c.start()
-        own_loc.start()
-
-    ahead_loc.start()
     incoming[2].wait()
     incoming[3].wait()
-    ahead_obs = remote(obs_v, prev_obs, sem_s.at[5], sem_r.at[2], after)
-    column_obs = [
-        remote(obs_v, col_obs, sem_s.at[5 + k], sem_r.at[3], {"grp": k, "dev": d})
-        for k in range(1, GRP)
-    ]
-    own_obs = pltpu.make_async_copy(obs_v, col_obs, sem_mine.at[1])
+
+    @pl.when(g == 0)
+    def _():
+        own_loc.wait()
+
+    @pl.when(g != 0)
+    def _():
+        column_loc[0].wait_recv()
+
+    mine_loc = local_copy(col_loc, all_loc.at[d], 2)
+    every_loc = spread(col_loc, all_loc, 9, 4)
     ahead_obs.start()
 
     @pl.when(g == 0)
@@ -206,18 +218,6 @@
     ahead_loc.wait()
     pts[0] = points(prev_loc)
     covariance(0, 0)
-
-    @pl.when(g == 0)
-    def _():
-        own_loc.wait()
-
-    @pl.when(g != 0)
-    def _():
-        column_loc[0].wait_recv()
-
-    mine_loc = local_copy(col_loc, all_loc.at[d], 2)
-    every_loc = spread(col_loc, all_loc, 9, 4)
-
     def inverse(k, jobs=()):
         jobs = list(jobs)
         r = eye - first * tiles[k, k]
@@ -241,11 +241,14 @@
         halves, left = split(x), left.astype(BF16)
         return x + (dot(halves[0], left) + dot(halves[1], left))
 
+    def product(a, b, dims, k):
+        return dot6(a, b, dims) if k == 0 else dot3(split(a), split(b), dims)
+
     def lower(i, k, inv):
-        low[i, k] = dot6(tiles[i, k], inv)
+        low[i, k] = product(tiles[i, k], inv, NN, k)
 
     def update(i, j, k):
-        tiles[i, j] = tiles[i, j] - dot6(low[i, k], tiles[j, k], NT)
+        tiles[i, j] = tiles[i, j] - product(low[i, k], tiles[j, k], NT, k)
 
     def put(k, value):
         high, rest = split(value)
@@ -254,8 +257,7 @@
 
     inv = inverse(0)
     covariance(3, 0)
-    low[3, 0] = dot6(tiles[3, 0], inv)
-    tiles[3, 3] = tiles[3, 3] - dot6(low[3, 0], tiles[3, 0], NT)
+    lower(3, 0, inv)
 
     @pl.when(g == 0)
     def _():
@@ -288,6 +290,9 @@
         covariance(2, 2)
         update(2, 2, 0)
 
+    def fifth():
+        update(3, 3, 0)
+
     def four():
         covariance(3, 1)
         update(3, 1, 0)
@@ -296,7 +301,7 @@
         covariance(3, 2)
         update(3, 2, 0)
 
-    inv1 = inverse(1, (one, two, three, four, five))
+    inv1 = inverse(1, (one, two, three, four, five, fifth))
     lower(2, 1, inv1)
     update(2, 2, 1)
 

time: 57.7 us -> 56.3 us (0.976)
  Pallas kernels: 56.3 us -> 54.9 us
    pallas_call x1, Pallas kernels: 56.3 us -> 54.9 us  [local(): pl.pallas_call(kernel, out_shape=jax.ShapeDtypeStruct((2, fields, points)...]
where the time goes in v6:
time: 56.3 us; the launch traced here: 56.2 us
  Pallas kernels  54.9 us (98%)
  between operations  0.64 us (1%)
  local copies, waits for them, and re-layouts  0.61 us (1%)
    pallas_call x1, Pallas kernels, local(): pl.pallas_call(kernel, out_shape=jax.ShapeDtypeStruct((2, fields, points)...  54.9 us

profile of v6, /device:TPU:0, one launch (start us, length us, event | category | flops | bytes accessed | tf_op | source)
XLA Modules:
  0.0 56.2 jit_solution(15585983981464333493)
XLA Ops:
  0.6 54.9 %shard_map.59 = f32[2,8,256]{2,1,0:T(8,128)S(1)} custom-call(s32[1,4]{1,0:T(1,128)} %near_hbm.1, f32[3,1,256]{2,1,0:T(1,128)} %bitcast.1, f32[1,8,256]{2,1,0:T(8,128)} %obs.1, f32[1,8,256]{2,1,0:T(8,128)} %noise.1), custom_call_target="tpu_custom_call" | custom-call | tf_op jit(solution)/shard_map/pallas_call | solution.py:477
  55.6 0.6 %fusion = (f32[1,8,256]{2,1,0:T(8,128)}, f32[1,8,256]{2,1,0:T(8,128)}) fusion(f32[2,8,256]{2,1,0:T(8,128)S(1)} %shard_map.59), kind=kLoop, calls=%fused_computation | loop fusion | bytes 32768 | tf_op jit(solution)/shard_map/slice | solution.py:504

commit v7 on v6

--- a/solution.py
+++ b/solution.py
@@ -220,35 +220,40 @@
     covariance(0, 0)
     def inverse(k, jobs=()):
         jobs = list(jobs)
-        r = eye - first * tiles[k, k]
-        x = (first * rows[0][0]) * (eye + r)
-        pair = split(r)
-        r = rows[0][0] * dot3(pair, pair) - rows[0][1] * eye
+        e = first * tiles[k, k]
+        x = (first * rows[0][0]) * (2.0 * eye - e)
+        pair = split(e)
+        e = rows[0][0] * (2.0 * e - dot3(pair, pair))
         for n, (a, c) in enumerate(rows[1:], 1):
-            pair, halves = split(r), split(x)
+            halves = split(x)
             if n < FULL:
+                pair = split(e)
                 moved, square = dot3(halves, pair), dot3(pair, pair)
             else:
-                moved = dot(halves[0], pair[0]) + dot(halves[1], pair[0])
-                square = dot(pair[0], pair[0])
+                r = (eye - e if n == FULL else r).astype(BF16)
+                moved, square = dot(halves[0], r) + dot(halves[1], r), dot(r, r)
             if jobs:
                 jobs.pop(0)()
-            x = a * (x + moved)
-            r = a * square - c * eye
-        left = eye - dot6(tiles[k, k], x)
+            if n < FULL:
+                x, e = a * (2.0 * x - moved), a * (2.0 * e - square)
+            else:
+                x, r = a * (x + moved), a * square - c * eye
+        left = eye - dot6(tiles[k, k], x) if k == 3 else None
         for job in jobs:
             job()
+        if k < 3:
+            return x
         halves, left = split(x), left.astype(BF16)
         return x + (dot(halves[0], left) + dot(halves[1], left))
 
-    def product(a, b, dims, k):
-        return dot6(a, b, dims) if k == 0 else dot3(split(a), split(b), dims)
-
     def lower(i, k, inv):
-        low[i, k] = product(tiles[i, k], inv, NN, k)
+        panel, pair = tiles[i, k], split(inv)
+        value = dot3(split(panel), pair)
+        left = panel - dot6(value, tiles[k, k])
+        low[i, k] = value + dot3(split(left), pair)
 
     def update(i, j, k):
-        tiles[i, j] = tiles[i, j] - product(low[i, k], tiles[j, k], NT, k)
+        tiles[i, j] = tiles[i, j] - dot3(split(low[i, k]), split(tiles[j, k]), NT)
 
     def put(k, value):
         high, rest = split(value)
@@ -315,10 +320,10 @@
         update(3, 3, 1)
 
     def nine():
-        low[2, 0] = dot6(low[2, 1], low[1, 0]) - low[2, 0]
+        low[2, 0] = dot3(split(low[2, 1]), split(low[1, 0])) - low[2, 0]
 
     def ten():
-        low[3, 0] = dot6(low[3, 1], low[1, 0]) - low[3, 0]
+        low[3, 0] = dot3(split(low[3, 1]), split(low[1, 0])) - low[3, 0]
 
     inv2 = inverse(2, (six, seven, eight, nine, ten))
     lower(3, 2, inv2)
@@ -328,10 +333,10 @@
         put(2, -low[3, 2])
 
     def twelve():
-        put(1, dot6(low[3, 2], low[2, 1]) - low[3, 1])
+        put(1, dot3(split(low[3, 2]), split(low[2, 1])) - low[3, 1])
 
     def thirteen():
-        put(0, low[3, 0] - dot6(low[3, 2], low[2, 0]))
+        put(0, low[3, 0] - dot3(split(low[3, 2]), split(low[2, 0])))
 
     def dot_small(rows, mat, dims):
         high, rest = split(rows)

time: 56.3 us -> 57.3 us (1.018)
  Pallas kernels: 54.9 us -> 56 us
    pallas_call x1, Pallas kernels: 54.9 us -> 56 us  [local(): pl.pallas_call(kernel, out_shape=jax.ShapeDtypeStruct((2, fields, points)...]
where the time goes in v7:
time: 57.3 us; the launch traced here: 57.2 us
  Pallas kernels  56 us (98%)
  between operations  0.64 us (1%)
  local copies, waits for them, and re-layouts  0.61 us (1%)
    pallas_call x1, Pallas kernels, local(): pl.pallas_call(kernel, out_shape=jax.ShapeDtypeStruct((2, fields, points)...  56 us

profile of v7, /device:TPU:0, one launch (start us, length us, event | category | flops | bytes accessed | tf_op | source)
XLA Modules:
  0.0 57.2 jit_solution(16924779557567292970)
XLA Ops:
  0.6 56.0 %shard_map.59 = f32[2,8,256]{2,1,0:T(8,128)S(1)} custom-call(s32[1,4]{1,0:T(1,128)} %near_hbm.1, f32[3,1,256]{2,1,0:T(1,128)} %bitcast.1, f32[1,8,256]{2,1,0:T(8,128)} %obs.1, f32[1,8,256]{2,1,0:T(8,128)} %noise.1), custom_call_target="tpu_custom_call" | custom-call | tf_op jit(solution)/shard_map/pallas_call | solution.py:482
  56.6 0.6 %fusion = (f32[1,8,256]{2,1,0:T(8,128)}, f32[1,8,256]{2,1,0:T(8,128)}) fusion(f32[2,8,256]{2,1,0:T(8,128)S(1)} %shard_map.59), kind=kLoop, calls=%fused_computation | loop fusion | bytes 32768 | tf_op jit(solution)/shard_map/slice | solution.py:509

commit v8 on v7

--- a/solution.py
+++ b/solution.py
@@ -263,6 +263,7 @@
     inv = inverse(0)
     covariance(3, 0)
     lower(3, 0, inv)
+    update(3, 3, 0)
 
     @pl.when(g == 0)
     def _():
@@ -295,9 +296,6 @@
         covariance(2, 2)
         update(2, 2, 0)
 
-    def fifth():
-        update(3, 3, 0)
-
     def four():
         covariance(3, 1)
         update(3, 1, 0)
@@ -306,7 +304,7 @@
         covariance(3, 2)
         update(3, 2, 0)
 
-    inv1 = inverse(1, (one, two, three, four, five, fifth))
+    inv1 = inverse(1, (one, two, three, four, five))
     lower(2, 1, inv1)
     update(2, 2, 1)
 

time: 57.3 us -> 57.1 us (level)
  no operation moved by 1% of the time
where the time goes in v8:
time: 57.1 us; the launch traced here: 56.9 us
  Pallas kernels  55.7 us (98%)
  between operations  0.64 us (1%)
  local copies, waits for them, and re-layouts  0.61 us (1%)
    pallas_call x1, Pallas kernels, local(): pl.pallas_call(kernel, out_shape=jax.ShapeDtypeStruct((2, fields, points)...  55.7 us

profile of v8, /device:TPU:0, one launch (start us, length us, event | category | flops | bytes accessed | tf_op | source)
XLA Modules:
  0.0 56.9 jit_solution(17641749304153129895)
XLA Ops:
  0.6 55.7 %shard_map.59 = f32[2,8,256]{2,1,0:T(8,128)S(1)} custom-call(s32[1,4]{1,0:T(1,128)} %near_hbm.1, f32[3,1,256]{2,1,0:T(1,128)} %bitcast.1, f32[1,8,256]{2,1,0:T(8,128)} %obs.1, f32[1,8,256]{2,1,0:T(8,128)} %noise.1), custom_call_target="tpu_custom_call" | custom-call | tf_op jit(solution)/shard_map/pallas_call | solution.py:480
  56.3 0.6 %fusion = (f32[1,8,256]{2,1,0:T(8,128)}, f32[1,8,256]{2,1,0:T(8,128)}) fusion(f32[2,8,256]{2,1,0:T(8,128)S(1)} %shard_map.59), kind=kLoop, calls=%fused_computation | loop fusion | bytes 32768 | tf_op jit(solution)/shard_map/slice | solution.py:507
